TPU v7x, 1024 devices: a whole 4x4x32 slice. The times are simulated.
1024 devices in a mesh: dom: 256 (over z, x, core), sub: 4 (over y).
Axes of the slice: x: 4, y: 4, z: 32, core: 2. Of those that a mesh axis runs over, the one named last changes fastest.
Arguments:
- rhs_local: float32 [2048, 128, 128], P('dom', 'sub'), may hold values from -8 to 8
- coefficient: float32 [2048, 128, 128], P('dom', 'sub'), may hold values from 0.3 to 3
Outputs:
- preconditioned: float32 [2048, 128, 128], P('dom', 'sub')
- coarse_solution: float32 [512, 32, 32], P('dom', 'sub')
All inputs are finite; a program needn't handle non-finite values.
Results may differ from a plain program's by a relative error of at most 0.0003.
Values sent between devices are 32-bit elements; how exact they have to be, the bound alone decides.
A program may use at most 64 MiB of HBM per device.

v0:
```python
import jax
import jax.numpy as jnp
import numpy as np
from jax import lax
from jax.sharding import PartitionSpec as P

EZ = 16


def extended(block, sides, width):
    for axis, dim in sides:
        count = lax.axis_size(axis)
        forward = [(i, i + 1) for i in range(count - 1)]
        backward = [(target, source) for source, target in forward]
        low = lax.ppermute(
            lax.slice_in_dim(block, block.shape[dim] - width, None, axis=dim), axis, forward
        )
        high = lax.ppermute(lax.slice_in_dim(block, 0, width, axis=dim), axis, backward)
        block = jnp.concatenate([low, block, high], axis=dim)
    return block


def legendre_value(points, degree):
    previous = np.ones(points.shape)
    current = points.copy()
    for level in range(1, degree):
        following = ((2 * level + 1) * points * current - level * previous) / (level + 1)
        previous = current
        current = following
    return current


def tables():
    degree = 7
    points = np.array(
        [
            -1.0,
            -0.8717401485096066,
            -0.5917001814331423,
            -0.2092992179024789,
            0.2092992179024789,
            0.5917001814331423,
            0.8717401485096066,
            1.0,
        ]
    )
    values = legendre_value(points, degree)
    weights = 2.0 / (degree * (degree + 1) * values**2)
    derivative = np.zeros((8, 8))
    for row_at in range(8):
        for col_at in range(8):
            if row_at != col_at:
                derivative[row_at, col_at] = values[row_at] / (
                    values[col_at] * (points[row_at] - points[col_at])
                )
    derivative[0, 0] = -degree * (degree + 1) / 4.0
    derivative[7, 7] = degree * (degree + 1) / 4.0
    interp = np.stack([(1.0 - points) / 2.0, (1.0 + points) / 2.0], axis=1)
    slopes = np.array([-0.5, 0.5])
    return (derivative, weights, interp, slopes)


def fold_local(field, axis_at, per_elem):
    dims_of = field.shape
    elements = dims_of[axis_at] // per_elem
    split = field.reshape(dims_of[:axis_at] + (elements, per_elem) + dims_of[axis_at + 1 :])
    first_face = lax.index_in_dim(split, 0, axis_at + 1, keepdims=False)
    last_face = lax.index_in_dim(split, per_elem - 1, axis_at + 1, keepdims=False)
    empty_face = jnp.zeros_like(lax.slice_in_dim(first_face, 0, 1, axis=axis_at))
    from_left = jnp.concatenate(
        [empty_face, lax.slice_in_dim(last_face, 0, elements - 1, axis=axis_at)], axis_at
    )
    from_right = jnp.concatenate(
        [lax.slice_in_dim(first_face, 1, elements, axis=axis_at), empty_face], axis_at
    )
    middle = lax.slice_in_dim(split, 1, per_elem - 1, axis=axis_at + 1)
    joined = jnp.concatenate(
        [
            jnp.expand_dims(first_face + from_left, axis_at + 1),
            middle,
            jnp.expand_dims(last_face + from_right, axis_at + 1),
        ],
        axis_at + 1,
    )
    return joined.reshape(dims_of)


def fold_rim(padded, axis_at):
    length = padded.shape[axis_at] - 2
    inside = lax.slice_in_dim(padded, 1, length + 1, axis=axis_at)
    low_side = lax.slice_in_dim(inside, 0, 1, axis=axis_at) + lax.slice_in_dim(
        padded, 0, 1, axis=axis_at
    )
    high_side = lax.slice_in_dim(inside, length - 1, length, axis=axis_at) + lax.slice_in_dim(
        padded, length + 1, length + 2, axis=axis_at
    )
    return jnp.concatenate(
        [low_side, lax.slice_in_dim(inside, 1, length - 1, axis=axis_at), high_side], axis_at
    )


def assemble(stacked):
    local = fold_local(fold_local(fold_local(stacked, 1, 8), 2, 8), 3, 8)
    padded = extended(local, (("dom", 1), ("sub", 2)), 1)
    result = fold_rim(fold_rim(padded, 1), 2)
    return result


def coarse_assemble(stacked):
    local = fold_local(fold_local(fold_local(stacked, 1, 2), 2, 2), 3, 2)
    padded = extended(local, (("dom", 1), ("sub", 2)), 1)
    result = fold_rim(fold_rim(padded, 1), 2)
    return result


def edge_mask(length, start, total):
    spots = jnp.arange(length) + start
    return ((spots > 0) & (spots < total - 1)).astype(jnp.float32)


def weight_field(size_x, size_y, size_z, weights):
    wvec = jnp.asarray(weights, jnp.float32)
    along_x = jnp.tile(wvec, size_x // 8)
    along_y = jnp.tile(wvec, size_y // 8)
    along_z = jnp.tile(wvec, size_z // 8)
    return along_x[:, None, None] * along_y[None, :, None] * along_z[None, None, :]


def local_operator(field, weighted, derivative, z_matrix):
    size_x, size_y, size_z = field.shape
    precise = lax.Precision.HIGHEST
    z_block = z_matrix.shape[0]
    grad_x = jnp.einsum(
        "ab,ebyz->eayz",
        derivative,
        field.reshape(size_x // 8, 8, size_y, size_z),
        precision=precise,
    ).reshape(field.shape)
    grad_y = jnp.einsum(
        "ab,xebz->xeaz",
        derivative,
        field.reshape(size_x, size_y // 8, 8, size_z),
        precision=precise,
    ).reshape(field.shape)
    grad_z = jnp.dot(
        field.reshape(-1, z_block),
        z_matrix.T,
        precision=precise,
        preferred_element_type=jnp.float32,
    ).reshape(field.shape)
    flux_x = (weighted * grad_x).reshape(size_x // 8, 8, size_y, size_z)
    flux_y = (weighted * grad_y).reshape(size_x, size_y // 8, 8, size_z)
    flux_z = (weighted * grad_z).reshape(-1, z_block)
    back_x = jnp.einsum("ab,eayz->ebyz", derivative, flux_x, precision=precise).reshape(field.shape)
    back_y = jnp.einsum("ab,xeaz->xebz", derivative, flux_y, precision=precise).reshape(field.shape)
    back_z = jnp.dot(
        flux_z, z_matrix, precision=precise, preferred_element_type=jnp.float32
    ).reshape(field.shape)
    return back_x + back_y + back_z


def diagonal_local(weighted, derivative, z_matrix):
    size_x, size_y, size_z = weighted.shape
    precise = lax.Precision.HIGHEST
    squared = derivative * derivative
    z_block = z_matrix.shape[0]
    part_x = jnp.einsum(
        "ka,ekyz->eayz",
        squared,
        weighted.reshape(size_x // 8, 8, size_y, size_z),
        precision=precise,
    ).reshape(weighted.shape)
    part_y = jnp.einsum(
        "ka,xekz->xeaz",
        squared,
        weighted.reshape(size_x, size_y // 8, 8, size_z),
        precision=precise,
    ).reshape(weighted.shape)
    part_z = jnp.dot(
        weighted.reshape(-1, z_block),
        z_matrix * z_matrix,
        precision=precise,
        preferred_element_type=jnp.float32,
    ).reshape(weighted.shape)
    return part_x + part_y + part_z


def restrict(field, interp):
    size_x, size_y, size_z = field.shape
    precise = lax.Precision.HIGHEST
    section_x = jnp.einsum(
        "ai,eayz->eiyz", interp, field.reshape(size_x // 8, 8, size_y, size_z), precision=precise
    ).reshape(size_x // 4, size_y, size_z)
    section_y = jnp.einsum(
        "ai,xeaz->xeiz",
        interp,
        section_x.reshape(size_x // 4, size_y // 8, 8, size_z),
        precision=precise,
    ).reshape(size_x // 4, size_y // 4, size_z)
    section_z = jnp.einsum(
        "ai,xyea->xyei",
        interp,
        section_y.reshape(size_x // 4, size_y // 4, size_z // 8, 8),
        precision=precise,
    )
    return section_z.reshape(size_x // 4, size_y // 4, size_z // 4)


def prolong(coarse, interp):
    size_x, size_y, size_z = coarse.shape
    precise = lax.Precision.HIGHEST
    section_z = jnp.einsum(
        "ai,xyei->xyea", interp, coarse.reshape(size_x, size_y, size_z // 2, 2), precision=precise
    ).reshape(size_x, size_y, size_z * 4)
    section_y = jnp.einsum(
        "ai,xeiz->xeaz",
        interp,
        section_z.reshape(size_x, size_y // 2, 2, size_z * 4),
        precision=precise,
    ).reshape(size_x, size_y * 4, size_z * 4)
    section_x = jnp.einsum(
        "ai,eiyz->eayz",
        interp,
        section_y.reshape(size_x // 2, 2, size_y * 4, size_z * 4),
        precision=precise,
    )
    return section_x.reshape(size_x * 4, size_y * 4, size_z * 4)


def coarse_matrices(weighted, interp, slopes):
    size_x, size_y, size_z = weighted.shape
    precise = lax.Precision.HIGHEST
    shaped = weighted.reshape(size_x // 8, 8, size_y // 8, 8, size_z // 8, 8)
    interp_t = interp.T
    mass_pair = jnp.asarray(interp_t[:, None, :] * interp_t[None, :, :], jnp.float32)
    grad_pair = jnp.asarray(
        slopes[:, None, None] * slopes[None, :, None] * np.ones((1, 1, 8)), jnp.float32
    )
    form = "xaybzc,ipa,jqb,krc->ijkpqrxyz"
    total = jnp.einsum(form, shaped, grad_pair, mass_pair, mass_pair, precision=precise)
    total = total + jnp.einsum(form, shaped, mass_pair, grad_pair, mass_pair, precision=precise)
    total = total + jnp.einsum(form, shaped, mass_pair, mass_pair, grad_pair, precision=precise)
    return total.reshape(8, 8, -1)


def coarse_diagonal(galerkin, ex_n, ey_n, ez_n):
    eye_table = jnp.eye(8, dtype=jnp.float32)
    flat = jnp.sum(galerkin * eye_table[:, :, None], axis=1)
    return (
        flat.reshape(2, 2, 2, ex_n, ey_n, ez_n)
        .transpose(3, 0, 4, 1, 5, 2)
        .reshape(2 * ex_n, 2 * ey_n, 2 * ez_n)
    )


def coarse_apply(galerkin, coarse):
    size_x, size_y, size_z = coarse.shape
    ex_n, ey_n, ez_n = (size_x // 2, size_y // 2, size_z // 2)
    flat = coarse.reshape(ex_n, 2, ey_n, 2, ez_n, 2).transpose(1, 3, 5, 0, 2, 4).reshape(8, -1)
    result = jnp.sum(galerkin * flat[None, :, :], axis=1)
    return (
        result.reshape(2, 2, 2, ex_n, ey_n, ez_n).transpose(3, 0, 4, 1, 5, 2).reshape(coarse.shape)
    )


def shards(rhs_local, coefficient):
    derivative_np, weights, interp_np, slopes = tables()
    derivative = jnp.asarray(derivative_np, jnp.float32)
    interp = jnp.asarray(interp_np, jnp.float32)
    z_block = min(EZ, 16)
    z_matrix = jnp.asarray(np.kron(np.eye(z_block), derivative_np), jnp.float32)
    size_x, size_y, size_z = rhs_local.shape
    dom_count = lax.axis_size("dom")
    sub_count = lax.axis_size("sub")
    dom_index = lax.axis_index("dom")
    sub_index = lax.axis_index("sub")
    weighted = coefficient * weight_field(size_x, size_y, size_z, weights)
    fmask = (
        edge_mask(size_x, dom_index * size_x, size_x * dom_count)[:, None, None]
        * edge_mask(size_y, sub_index * size_y, size_y * sub_count)[None, :, None]
        * edge_mask(size_z, 0, size_z)[None, None, :]
    )

    def operate(field):
        return fmask * assemble(local_operator(field, weighted, derivative, z_matrix)[None])[0]

    summed = assemble(jnp.stack([rhs_local, diagonal_local(weighted, derivative, z_matrix)]))
    residual = fmask * summed[0]
    inverse = fmask / summed[1]
    theta = 1.1
    delta = 0.9
    sigma_val = theta / delta
    rho_prev = 1.0 / sigma_val
    rho_next = 1.0 / (2.0 * sigma_val - rho_prev)
    step_one = inverse * residual / theta
    res_one = residual - operate(step_one)
    second = step_one + rho_next * rho_prev * step_one + 2.0 * rho_next / delta * inverse * res_one
    res_two = residual - operate(second)
    elem_x, elem_y, elem_z = (size_x // 8, size_y // 8, size_z // 8)
    galerkin = coarse_matrices(weighted, interp_np, slopes)
    coarse_stack = jnp.stack(
        [restrict(res_two, interp), coarse_diagonal(galerkin, elem_x, elem_y, elem_z)]
    )
    own_y = coarse_stack.shape[2]
    y_start = sub_index * own_y
    coarse_x, coarse_y, coarse_z = coarse_stack.shape[1:]
    cmask = (
        edge_mask(coarse_x, dom_index * coarse_x, coarse_x * dom_count)[:, None, None]
        * edge_mask(coarse_y, y_start, own_y * sub_count)[None, :, None]
        * edge_mask(coarse_z, 0, coarse_z)[None, None, :]
    )
    assembled = coarse_assemble(coarse_stack)
    coarse_rhs = cmask * assembled[0]
    coarse_diag = assembled[1]
    coarse_one = 2.0 / 3.0 * coarse_rhs / coarse_diag
    image_c = cmask * coarse_assemble(coarse_apply(galerkin, coarse_one)[None])[0]
    coarse_solution = coarse_one + 2.0 / 3.0 * (coarse_rhs - image_c) / coarse_diag
    preconditioned = second + fmask * prolong(coarse_solution, interp)
    return (preconditioned, coarse_solution)


def solution(mesh):
    return jax.shard_map(
        shards,
        mesh=mesh,
        in_specs=(P("dom", "sub", None), P("dom", "sub", None)),
        out_specs=(P("dom", "sub", None), P("dom", "sub", None)),
        check_vma=False,
    )
```

profile of v0, /device:TPU:103, one launch (start us, length us, event | category | flops | bytes accessed | tf_op | source)
XLA Modules:
  0.0 190.2 jit_solution(17348411617119983382)
XLA Ops:
  8.3 3.7 %reshape_reshape.36 = f32[2,8,32,16,8]{4,3,2,1,0:T(8,128)} reshape(f32[2,8,4,8,128]{4,3,2,1,0:T(8,128)S(1)} %pad_maximum_fusion.4) | data formatting | bytes 524288 | tf_op jit(solution)/shard_map/reshape;reshape | solution.py:66
  12.1 8.2 %fusion.126 = (f32[2,8,32,16,1]{4,3,2,1,0:T(8,128)}, f32[2,8,32,16,1]{4,3,2,1,0:T(8,128)}) fusion(f32[2,8,32,16,8]{4,3,2,1,0:T(8,128)} %reshape_reshape.36), kind=kLoop, calls=%fused_computation.281 | loop fusion | bytes 131072 | tf_op jit(solution)/shard_map/slice | solution.py:68
  20.3 3.2 %slice.536 = f32[2,8,32,16,6]{4,3,2,1,0:T(8,128)} slice(f32[2,8,32,16,8]{4,3,2,1,0:T(8,128)S(1)} %copy-done), slice={[0:2], [0:8], [0:32], [0:16], [1:7]} | slice | bytes 393216 | tf_op jit(solution)/shard_map/slice | solution.py:76
  23.5 3.3 %copy.530 = f32[2,8,32,16,1]{2,3,4,1,0:T(8,128)S(1)} copy(f32[2,8,32,16,1]{4,3,2,1,0:T(8,128)} %get-tuple-element.22) | data formatting | bytes 65536 | tf_op jit(solution)/shard_map/slice | solution.py:68
  26.7 3.3 %copy.529 = f32[2,8,32,16,1]{2,3,4,1,0:T(8,128)S(1)} copy(f32[2,8,32,16,1]{4,3,2,1,0:T(8,128)} %get-tuple-element.23) | data formatting | bytes 65536 | tf_op jit(solution)/shard_map/slice | solution.py:67
  30.1 3.4 %copy.532 = f32[2,8,32,16,6]{2,4,3,1,0:T(8,128)S(1)} copy(f32[2,8,32,16,6]{4,3,2,1,0:T(8,128)} %slice.536) | data formatting | bytes 393216 | tf_op jit(solution)/shard_map/slice | solution.py:76
  35.0 5.2 %collective-permute-start = (f32[2,1,32,128]{3,1,2,0:T(1,128)}, f32[2,1,32,128]{3,1,2,0:T(1,128)}, u32[]{:S(2)}, u32[]{:S(2)}) collective-permute-start(f32[2,1,32,128]{3,1,2,0:T(1,128)} %get-tuple-element.34), channel_id=1, source_target_pairs={{0,4},{4,8},{8,12},{12,16},{16,20},{20,24},{24,28},{28,32},{32,36}... | collective-permute-start | bytes 98312 | tf_op jit(solution)/shard_map/ppermute | solution.py:15
  56.0 3.2 %collective-permute-start.2 = (f32[2,10,1,128]{3,1,2,0:T(8,128)S(1)}, f32[2,10,1,128]{3,1,2,0:T(8,128)S(1)}, u32[]{:S(2)}, u32[]{:S(2)}) collective-permute-start(f32[2,10,1,128]{3,1,2,0:T(8,128)S(1)} %get-tuple-element.30), channel_id=1, source_target_pairs={{0,1},{1,2},{2,3},{4,5},{5,6},{6,7},{8,9},{9,10},{10,11},{12,13},{... | collective-permute-start | bytes 30728 | tf_op jit(solution)/shard_map/ppermute | solution.py:15
  60.8 3.0 %collective-permute-done.3 = f32[2,10,1,128]{3,1,2,0:T(8,128)S(1)} collective-permute-done((f32[2,10,1,128]{3,1,2,0:T(8,128)S(1)}, f32[2,10,1,128]{3,1,2,0:T(8,128)S(1)}, u32[]{:S(2)}, u32[]{:S(2)}) %collective-permute-start.3) | collective-permute-done | bytes 10272 | tf_op jit(solution)/shard_map/ppermute | solution.py:18
  71.1 2.7 %fusion.128 = (f32[1,8,32,16,1]{4,3,2,1,0:T(8,128)}, f32[1,8,32,16,1]{4,3,2,1,0:T(8,128)}) fusion(f32[1,8,32,16,8]{4,3,2,1,0:T(8,128)S(1)} %reshape_reshape.38), kind=kLoop, calls=%fused_computation.283 | loop fusion | bytes 65536 | tf_op jit(solution)/shard_map/slice | solution.py:68
  75.7 2.6 %copy.551 = f32[1,8,32,16,1]{2,3,4,1,0:T(8,128)S(1)} copy(f32[1,8,32,16,1]{4,3,2,1,0:T(8,128)} %get-tuple-element.26) | data formatting | bytes 32768 | tf_op jit(solution)/shard_map/slice | solution.py:68
  84.1 8.4 %collective-permute-start.4 = (f32[1,1,32,128]{3,1,2,0:T(1,128)S(1)}, f32[1,1,32,128]{3,1,2,0:T(1,128)S(1)}, u32[]{:S(2)}, u32[]{:S(2)}) collective-permute-start(f32[1,1,32,128]{3,1,2,0:T(1,128)S(1)} %get-tuple-element.54), channel_id=1, source_target_pairs={{0,4},{4,8},{8,12},{12,16},{16,20},{20,24},{24,28},{28,32},{32,36}... | collective-permute-start | bytes 49160 | tf_op jit(solution)/shard_map/ppermute | solution.py:15
  94.5 6.4 %collective-permute-done.5 = f32[1,1,32,128]{3,1,2,0:T(1,128)S(1)} collective-permute-done((f32[1,1,32,128]{3,1,2,0:T(1,128)S(1)}, f32[1,1,32,128]{3,1,2,0:T(1,128)S(1)}, u32[]{:S(2)}, u32[]{:S(2)}) %collective-permute-start.5) | collective-permute-done | bytes 16416 | tf_op jit(solution)/shard_map/ppermute | solution.py:18
  100.9 3.2 %collective-permute-start.6 = (f32[1,10,1,128]{3,1,2,0:T(8,128)S(1)}, f32[1,10,1,128]{3,1,2,0:T(8,128)S(1)}, u32[]{:S(2)}, u32[]{:S(2)}) collective-permute-start(f32[1,10,1,128]{3,1,2,0:T(8,128)S(1)} %get-tuple-element.46), channel_id=1, source_target_pairs={{0,1},{1,2},{2,3},{4,5},{5,6},{6,7},{8,9},{9,10},{10,11},{12,13},{... | collective-permute-start | bytes 15368 | tf_op jit(solution)/shard_map/ppermute | solution.py:15
  112.7 2.7 %fusion.127 = (f32[1,8,32,16,1]{4,3,2,1,0:T(8,128)}, f32[1,8,32,16,1]{4,3,2,1,0:T(8,128)}) fusion(f32[1,8,32,16,8]{4,3,2,1,0:T(8,128)S(1)} %reshape_reshape.40), kind=kLoop, calls=%fused_computation.282 | loop fusion | bytes 65536 | tf_op jit(solution)/shard_map/slice | solution.py:68
  126.0 3.4 %collective-permute-start.8 = (f32[1,1,32,128]{3,1,2,0:T(1,128)S(1)}, f32[1,1,32,128]{3,1,2,0:T(1,128)S(1)}, u32[]{:S(2)}, u32[]{:S(2)}) collective-permute-start(f32[1,1,32,128]{3,1,2,0:T(1,128)S(1)} %get-tuple-element.50), channel_id=1, source_target_pairs={{0,4},{4,8},{8,12},{12,16},{16,20},{20,24},{24,28},{28,32},{32,36}... | collective-permute-start | bytes 49160 | tf_op jit(solution)/shard_map/ppermute | solution.py:15
  133.0 4.7 %collective-permute-done.9 = f32[1,1,32,128]{3,1,2,0:T(1,128)S(1)} collective-permute-done((f32[1,1,32,128]{3,1,2,0:T(1,128)S(1)}, f32[1,1,32,128]{3,1,2,0:T(1,128)S(1)}, u32[]{:S(2)}, u32[]{:S(2)}) %collective-permute-start.9) | collective-permute-done | bytes 16416 | tf_op jit(solution)/shard_map/ppermute | solution.py:18
  137.7 2.9 %collective-permute-start.10 = (f32[1,10,1,128]{3,1,2,0:T(8,128)S(1)}, f32[1,10,1,128]{3,1,2,0:T(8,128)S(1)}, u32[]{:S(2)}, u32[]{:S(2)}) collective-permute-start(f32[1,10,1,128]{3,1,2,0:T(8,128)S(1)} %get-tuple-element.44), channel_id=1, source_target_pairs={{0,1},{1,2},{2,3},{4,5},{5,6},{6,7},{8,9},{9,10},{10,11},{12,13},{... | collective-permute-start | bytes 15368 | tf_op jit(solution)/shard_map/ppermute | solution.py:15
  147.2 3.7 %collective-permute-start.12 = (f32[2,1,8,32]{2,3,1,0:T(8,128)S(1)}, f32[2,1,8,32]{2,3,1,0:T(8,128)S(1)}, u32[]{:S(2)}, u32[]{:S(2)}) collective-permute-start(f32[2,1,8,32]{2,3,1,0:T(8,128)S(1)} %get-tuple-element.64), channel_id=1, source_target_pairs={{0,4},{4,8},{8,12},{12,16},{16,20},{20,24},{24,28},{28,32},{32,36}... | collective-permute-start | bytes 6152 | tf_op jit(solution)/shard_map/ppermute | solution.py:15
  152.8 6.6 %collective-permute-done.13 = f32[2,1,8,32]{2,3,1,0:T(8,128)S(1)} collective-permute-done((f32[2,1,8,32]{2,3,1,0:T(8,128)S(1)}, f32[2,1,8,32]{2,3,1,0:T(8,128)S(1)}, u32[]{:S(2)}, u32[]{:S(2)}) %collective-permute-start.13) | collective-permute-done | bytes 2080 | tf_op jit(solution)/shard_map/ppermute | solution.py:18
  163.2 3.7 %collective-permute-done.15 = f32[2,4,1,32]{2,3,1,0:T(8,128)S(1)} collective-permute-done((f32[2,4,1,32]{2,3,1,0:T(8,128)S(1)}, f32[2,4,1,32]{2,3,1,0:T(8,128)S(1)}, u32[]{:S(2)}, u32[]{:S(2)}) %collective-permute-start.15) | collective-permute-done | bytes 1056 | tf_op jit(solution)/shard_map/ppermute | solution.py:18
  168.8 3.3 %collective-permute-start.16 = (f32[1,1,8,32]{2,3,1,0:T(8,128)S(1)}, f32[1,1,8,32]{2,3,1,0:T(8,128)S(1)}, u32[]{:S(2)}, u32[]{:S(2)}) collective-permute-start(f32[1,1,8,32]{2,3,1,0:T(8,128)S(1)} %get-tuple-element.68), channel_id=1, source_target_pairs={{0,4},{4,8},{8,12},{12,16},{16,20},{20,24},{24,28},{28,32},{32,36}... | collective-permute-start | bytes 3080 | tf_op jit(solution)/shard_map/ppermute | solution.py:15
  174.2 6.4 %collective-permute-done.17 = f32[1,1,8,32]{2,3,1,0:T(8,128)S(1)} collective-permute-done((f32[1,1,8,32]{2,3,1,0:T(8,128)S(1)}, f32[1,1,8,32]{2,3,1,0:T(8,128)S(1)}, u32[]{:S(2)}, u32[]{:S(2)}) %collective-permute-start.17) | collective-permute-done | bytes 1056 | tf_op jit(solution)/shard_map/ppermute | solution.py:18
  183.9 3.4 %collective-permute-done.19 = f32[1,4,1,32]{2,3,1,0:T(8,128)S(1)} collective-permute-done((f32[1,4,1,32]{2,3,1,0:T(8,128)S(1)}, f32[1,4,1,32]{2,3,1,0:T(8,128)S(1)}, u32[]{:S(2)}, u32[]{:S(2)}) %collective-permute-start.19) | collective-permute-done | bytes 544 | tf_op jit(solution)/shard_map/ppermute | solution.py:18
  (311 shorter events, 87.2 us)
Async XLA Ops:
  35.0 20.3 %collective-permute-start = (f32[2,1,32,128]{3,1,2,0:T(1,128)}, f32[2,1,32,128]{3,1,2,0:T(1,128)}, u32[]{:S(2)}, u32[]{:S(2)}) collective-permute-start(f32[2,1,32,128]{3,1,2,0:T(1,128)} %get-tuple-element.34), channel_id=1, source_target_pairs={{0,4},{4,8},{8,12},{12,16},{16,20},{20,24},{24,28},{28,32},{32,36}... | collective-permute-start | bytes 98312 | tf_op jit(solution)/shard_map/ppermute | solution.py:15
  40.2 15.1 %collective-permute-start.1 = (f32[2,1,32,128]{3,1,2,0:T(1,128)}, f32[2,1,32,128]{3,1,2,0:T(1,128)}, u32[]{:S(2)}, u32[]{:S(2)}) collective-permute-start(f32[2,1,32,128]{3,1,2,0:T(1,128)} %get-tuple-element.35), channel_id=1, source_target_pairs={{4,0},{8,4},{12,8},{16,12},{20,16},{24,20},{28,24},{32,28},{36,32}... | collective-permute-start | bytes 98312 | tf_op jit(solution)/shard_map/ppermute | solution.py:18
  56.0 4.8 %collective-permute-start.2 = (f32[2,10,1,128]{3,1,2,0:T(8,128)S(1)}, f32[2,10,1,128]{3,1,2,0:T(8,128)S(1)}, u32[]{:S(2)}, u32[]{:S(2)}) collective-permute-start(f32[2,10,1,128]{3,1,2,0:T(8,128)S(1)} %get-tuple-element.30), channel_id=1, source_target_pairs={{0,1},{1,2},{2,3},{4,5},{5,6},{6,7},{8,9},{9,10},{10,11},{12,13},{... | collective-permute-start | bytes 30728 | tf_op jit(solution)/shard_map/ppermute | solution.py:15
  59.2 4.6 %collective-permute-start.3 = (f32[2,10,1,128]{3,1,2,0:T(8,128)S(1)}, f32[2,10,1,128]{3,1,2,0:T(8,128)S(1)}, u32[]{:S(2)}, u32[]{:S(2)}) collective-permute-start(f32[2,10,1,128]{3,1,2,0:T(8,128)S(1)} %get-tuple-element.31), channel_id=1, source_target_pairs={{1,0},{2,1},{3,2},{5,4},{6,5},{7,6},{9,8},{10,9},{11,10},{13,12},{... | collective-permute-start | bytes 30728 | tf_op jit(solution)/shard_map/ppermute | solution.py:18
  82.6 26.3 %copy-start.8 = (f32[8,32]{0,1:T(8,128)S(1)}, f32[8,32]{0,1:T(8,128)}, u32[]{:S(2)}) copy-start(f32[8,32]{0,1:T(8,128)} %broadcast_multiply_fusion.2) | copy-start | bytes 3076
  82.6 26.3 %copy-start.17 = (f32[8,8,1]{1,0,2:T(8,128)S(1)}, f32[8,8,1]{1,0,2:T(8,128)}, u32[]{:S(2)}) copy-start(f32[8,8,1]{1,0,2:T(8,128)} %constant.124) | copy-start | bytes 772
  82.6 26.3 %copy-start.33 = (f32[128]{0:T(128)S(1)}, f32[128]{0:T(128)}, u32[]{:S(2)}) copy-start(f32[128]{0:T(128)} %copy-done.32) | copy-start | bytes 1540
  84.1 10.4 %collective-permute-start.4 = (f32[1,1,32,128]{3,1,2,0:T(1,128)S(1)}, f32[1,1,32,128]{3,1,2,0:T(1,128)S(1)}, u32[]{:S(2)}, u32[]{:S(2)}) collective-permute-start(f32[1,1,32,128]{3,1,2,0:T(1,128)S(1)} %get-tuple-element.54), channel_id=1, source_target_pairs={{0,4},{4,8},{8,12},{12,16},{16,20},{20,24},{24,28},{28,32},{32,36}... | collective-permute-start | bytes 49160 | tf_op jit(solution)/shard_map/ppermute | solution.py:15
  92.5 8.4 %collective-permute-start.5 = (f32[1,1,32,128]{3,1,2,0:T(1,128)S(1)}, f32[1,1,32,128]{3,1,2,0:T(1,128)S(1)}, u32[]{:S(2)}, u32[]{:S(2)}) collective-permute-start(f32[1,1,32,128]{3,1,2,0:T(1,128)S(1)} %get-tuple-element.55), channel_id=1, source_target_pairs={{4,0},{8,4},{12,8},{16,12},{20,16},{24,20},{28,24},{32,28},{36,32}... | collective-permute-start | bytes 49160 | tf_op jit(solution)/shard_map/ppermute | solution.py:18
  100.9 5.4 %collective-permute-start.6 = (f32[1,10,1,128]{3,1,2,0:T(8,128)S(1)}, f32[1,10,1,128]{3,1,2,0:T(8,128)S(1)}, u32[]{:S(2)}, u32[]{:S(2)}) collective-permute-start(f32[1,10,1,128]{3,1,2,0:T(8,128)S(1)} %get-tuple-element.46), channel_id=1, source_target_pairs={{0,1},{1,2},{2,3},{4,5},{5,6},{6,7},{8,9},{9,10},{10,11},{12,13},{... | collective-permute-start | bytes 15368 | tf_op jit(solution)/shard_map/ppermute | solution.py:15
  104.1 4.4 %collective-permute-start.7 = (f32[1,10,1,128]{3,1,2,0:T(8,128)S(1)}, f32[1,10,1,128]{3,1,2,0:T(8,128)S(1)}, u32[]{:S(2)}, u32[]{:S(2)}) collective-permute-start(f32[1,10,1,128]{3,1,2,0:T(8,128)S(1)} %get-tuple-element.47), channel_id=1, source_target_pairs={{1,0},{2,1},{3,2},{5,4},{6,5},{7,6},{9,8},{10,9},{11,10},{13,12},{... | collective-permute-start | bytes 15368 | tf_op jit(solution)/shard_map/ppermute | solution.py:18
  126.0 7.0 %collective-permute-start.8 = (f32[1,1,32,128]{3,1,2,0:T(1,128)S(1)}, f32[1,1,32,128]{3,1,2,0:T(1,128)S(1)}, u32[]{:S(2)}, u32[]{:S(2)}) collective-permute-start(f32[1,1,32,128]{3,1,2,0:T(1,128)S(1)} %get-tuple-element.50), channel_id=1, source_target_pairs={{0,4},{4,8},{8,12},{12,16},{16,20},{20,24},{24,28},{28,32},{32,36}... | collective-permute-start | bytes 49160 | tf_op jit(solution)/shard_map/ppermute | solution.py:15
  129.3 8.4 %collective-permute-start.9 = (f32[1,1,32,128]{3,1,2,0:T(1,128)S(1)}, f32[1,1,32,128]{3,1,2,0:T(1,128)S(1)}, u32[]{:S(2)}, u32[]{:S(2)}) collective-permute-start(f32[1,1,32,128]{3,1,2,0:T(1,128)S(1)} %get-tuple-element.51), channel_id=1, source_target_pairs={{4,0},{8,4},{12,8},{16,12},{20,16},{24,20},{28,24},{32,28},{36,32}... | collective-permute-start | bytes 49160 | tf_op jit(solution)/shard_map/ppermute | solution.py:18
  137.7 5.1 %collective-permute-start.10 = (f32[1,10,1,128]{3,1,2,0:T(8,128)S(1)}, f32[1,10,1,128]{3,1,2,0:T(8,128)S(1)}, u32[]{:S(2)}, u32[]{:S(2)}) collective-permute-start(f32[1,10,1,128]{3,1,2,0:T(8,128)S(1)} %get-tuple-element.44), channel_id=1, source_target_pairs={{0,1},{1,2},{2,3},{4,5},{5,6},{6,7},{8,9},{9,10},{10,11},{12,13},{... | collective-permute-start | bytes 15368 | tf_op jit(solution)/shard_map/ppermute | solution.py:15
  140.6 4.4 %collective-permute-start.11 = (f32[1,10,1,128]{3,1,2,0:T(8,128)S(1)}, f32[1,10,1,128]{3,1,2,0:T(8,128)S(1)}, u32[]{:S(2)}, u32[]{:S(2)}) collective-permute-start(f32[1,10,1,128]{3,1,2,0:T(8,128)S(1)} %get-tuple-element.45), channel_id=1, source_target_pairs={{1,0},{2,1},{3,2},{5,4},{6,5},{7,6},{9,8},{10,9},{11,10},{13,12},{... | collective-permute-start | bytes 15368 | tf_op jit(solution)/shard_map/ppermute | solution.py:18
  147.0 27.1 %copy-start.36 = (f32[2]{0:T(128)S(1)}, f32[2]{0:T(128)}, u32[]{:S(2)}) copy-start(f32[2]{0:T(128)} %copy-done.35) | copy-start | bytes 28
  147.2 5.7 %collective-permute-start.12 = (f32[2,1,8,32]{2,3,1,0:T(8,128)S(1)}, f32[2,1,8,32]{2,3,1,0:T(8,128)S(1)}, u32[]{:S(2)}, u32[]{:S(2)}) collective-permute-start(f32[2,1,8,32]{2,3,1,0:T(8,128)S(1)} %get-tuple-element.64), channel_id=1, source_target_pairs={{0,4},{4,8},{8,12},{12,16},{16,20},{20,24},{24,28},{28,32},{32,36}... | collective-permute-start | bytes 6152 | tf_op jit(solution)/shard_map/ppermute | solution.py:15
  150.9 8.6 %collective-permute-start.13 = (f32[2,1,8,32]{2,3,1,0:T(8,128)S(1)}, f32[2,1,8,32]{2,3,1,0:T(8,128)S(1)}, u32[]{:S(2)}, u32[]{:S(2)}) collective-permute-start(f32[2,1,8,32]{2,3,1,0:T(8,128)S(1)} %get-tuple-element.65), channel_id=1, source_target_pairs={{4,0},{8,4},{12,8},{16,12},{20,16},{24,20},{28,24},{32,28},{36,32}... | collective-permute-start | bytes 6152 | tf_op jit(solution)/shard_map/ppermute | solution.py:18
  159.6 3.6 %collective-permute-start.14 = (f32[2,4,1,32]{2,3,1,0:T(8,128)S(1)}, f32[2,4,1,32]{2,3,1,0:T(8,128)S(1)}, u32[]{:S(2)}, u32[]{:S(2)}) collective-permute-start(f32[2,4,1,32]{2,3,1,0:T(8,128)S(1)} %get-tuple-element.48), channel_id=1, source_target_pairs={{0,1},{1,2},{2,3},{4,5},{5,6},{6,7},{8,9},{9,10},{10,11},{12,13},{... | collective-permute-start | bytes 3080 | tf_op jit(solution)/shard_map/ppermute | solution.py:15
  161.2 5.7 %collective-permute-start.15 = (f32[2,4,1,32]{2,3,1,0:T(8,128)S(1)}, f32[2,4,1,32]{2,3,1,0:T(8,128)S(1)}, u32[]{:S(2)}, u32[]{:S(2)}) collective-permute-start(f32[2,4,1,32]{2,3,1,0:T(8,128)S(1)} %get-tuple-element.49), channel_id=1, source_target_pairs={{1,0},{2,1},{3,2},{5,4},{6,5},{7,6},{9,8},{10,9},{11,10},{13,12},{... | collective-permute-start | bytes 3080 | tf_op jit(solution)/shard_map/ppermute | solution.py:18
  168.8 5.4 %collective-permute-start.16 = (f32[1,1,8,32]{2,3,1,0:T(8,128)S(1)}, f32[1,1,8,32]{2,3,1,0:T(8,128)S(1)}, u32[]{:S(2)}, u32[]{:S(2)}) collective-permute-start(f32[1,1,8,32]{2,3,1,0:T(8,128)S(1)} %get-tuple-element.68), channel_id=1, source_target_pairs={{0,4},{4,8},{8,12},{12,16},{16,20},{20,24},{24,28},{28,32},{32,36}... | collective-permute-start | bytes 3080 | tf_op jit(solution)/shard_map/ppermute | solution.py:15
  172.2 8.4 %collective-permute-start.17 = (f32[1,1,8,32]{2,3,1,0:T(8,128)S(1)}, f32[1,1,8,32]{2,3,1,0:T(8,128)S(1)}, u32[]{:S(2)}, u32[]{:S(2)}) collective-permute-start(f32[1,1,8,32]{2,3,1,0:T(8,128)S(1)} %get-tuple-element.69), channel_id=1, source_target_pairs={{4,0},{8,4},{12,8},{16,12},{20,16},{24,20},{28,24},{32,28},{36,32}... | collective-permute-start | bytes 3080 | tf_op jit(solution)/shard_map/ppermute | solution.py:18
  180.6 3.2 %collective-permute-start.18 = (f32[1,4,1,32]{2,3,1,0:T(8,128)S(1)}, f32[1,4,1,32]{2,3,1,0:T(8,128)S(1)}, u32[]{:S(2)}, u32[]{:S(2)}) collective-permute-start(f32[1,4,1,32]{2,3,1,0:T(8,128)S(1)} %get-tuple-element.58), channel_id=1, source_target_pairs={{0,1},{1,2},{2,3},{4,5},{5,6},{6,7},{8,9},{9,10},{10,11},{12,13},{... | collective-permute-start | bytes 1544 | tf_op jit(solution)/shard_map/ppermute | solution.py:15
  182.3 5.0 %collective-permute-start.19 = (f32[1,4,1,32]{2,3,1,0:T(8,128)S(1)}, f32[1,4,1,32]{2,3,1,0:T(8,128)S(1)}, u32[]{:S(2)}, u32[]{:S(2)}) collective-permute-start(f32[1,4,1,32]{2,3,1,0:T(8,128)S(1)} %get-tuple-element.59), channel_id=1, source_target_pairs={{1,0},{2,1},{3,2},{5,4},{6,5},{7,6},{9,8},{10,9},{11,10},{13,12},{... | collective-permute-start | bytes 1544 | tf_op jit(solution)/shard_map/ppermute | solution.py:18
  (35 other events, 368.8 us)
where the time goes:
time: 191 us; the launch traced here: 190 us
  local copies, waits for them, and re-layouts  60.8 us (32%)
  starting transfers between devices  53.4 us (28%)
  waiting for transfers between devices  39.1 us (20%)
  matrix products  18.7 us (10%)
  other arithmetic  15.9 us (8%)
  between operations  2.42 us (1%)
    ppermute x10, waiting for transfers between devices, extended(): lax.ppermute(lax.slice_in_dim(block, 0, width, axis=dim), axis, backward)  38.5 us
    ppermute x10, starting transfers between devices, extended(): lax.ppermute(lax.slice_in_dim(block, block.shape[dim] - width, None, axis...  36.6 us
    slice x9, local copies, waits for them, and re-layouts, fold_local(): lax.index_in_dim(split, per_elem - 1, axis_at + 1, keepdims=False)  22.2 us
    ppermute x10, starting transfers between devices, extended(): lax.ppermute(lax.slice_in_dim(block, 0, width, axis=dim), axis, backward)  16.7 us
    slice x10, local copies, waits for them, and re-layouts, fold_local(): middle = lax.slice_in_dim(split, 1, per_elem - 1, axis=axis_at + 1)  13.4 us
    slice x4, local copies, waits for them, and re-layouts, fold_local(): first_face = lax.index_in_dim(split, 0, axis_at + 1, keepdims=False)  8.43 us
    another operation x5, local copies, waits for them, and re-layouts, fold_local(): field.reshape(dims_of[:axis_at] + (elements, per_elem) + dims_of[axis_at...  6.27 us
    dot_general x3, matrix products, coarse_matrices(): jnp.einsum(form, shaped, mass_pair, grad_pair, mass_pair, precision=precise)  4.26 us
  transfers between devices with their start and end apart: 20, of which 10 were waited for; matrix products, arithmetic and copies ran while one was open for 9% of the time, Pallas kernels for 0%

commit v1 on v0

v1 whole, which is shorter than its diff:
```python
import functools

import jax
import jax.numpy as jnp
import numpy as np
from jax import lax
from jax.experimental import pallas as pl
from jax.experimental.pallas import tpu as pltpu
from jax.sharding import PartitionSpec as P

MESH = pl.DeviceIdType.MESH
HIGHEST = lax.Precision.HIGHEST
F32 = jnp.float32
BF16 = jnp.bfloat16

NEAR = [(dx, dy) for dx in (-1, 0, 1) for dy in (-1, 0, 1) if (dx, dy) != (0, 0)]
WIDE = [(dx, dy) for dx in (-2, -1, 0, 1, 2) for dy in (-1, 0, 1) if (dx, dy) != (0, 0)]
FAR = [pair for pair in WIDE if pair not in NEAR]
SIDE = [pair for pair in NEAR if pair[1] == 0]
ROWS = [pair for pair in NEAR if pair[0] == 0]
EDGE = [pair for pair in NEAR if pair[0] != 0 and pair[1] != 0]


def opposite(table, pair):
    return table.index((-pair[0], -pair[1]))


def tables():
    degree = 7
    points = np.array(
        [
            -1.0,
            -0.8717401485096066,
            -0.5917001814331423,
            -0.2092992179024789,
            0.2092992179024789,
            0.5917001814331423,
            0.8717401485096066,
            1.0,
        ]
    )
    previous = np.ones(points.shape)
    values = points.copy()
    for level in range(1, degree):
        following = ((2 * level + 1) * points * values - level * previous) / (level + 1)
        previous = values
        values = following
    weights = 2.0 / (degree * (degree + 1) * values**2)
    derivative = np.zeros((8, 8))
    for row_at in range(8):
        for col_at in range(8):
            if row_at != col_at:
                derivative[row_at, col_at] = values[row_at] / (
                    values[col_at] * (points[row_at] - points[col_at])
                )
    derivative[0, 0] = -degree * (degree + 1) / 4.0
    derivative[7, 7] = degree * (degree + 1) / 4.0
    interp = np.stack([(1.0 - points) / 2.0, (1.0 + points) / 2.0], axis=1)
    return derivative, weights, interp


DER, WTS, INT = tables()
MASS = [INT[:, 0] * INT[:, 0], INT[:, 0] * INT[:, 1], INT[:, 1] * INT[:, 1]]


def moment_maps(elements, order, slope):
    maps = np.zeros((len(order), elements + 1, 8 * elements))
    for at, offset in enumerate(order):
        for e in range(elements):
            nodes = slice(8 * e, 8 * e + 8)
            if offset == 0:
                maps[at, e, nodes] += 0.25 if slope else MASS[0]
                maps[at, e + 1, nodes] += 0.25 if slope else MASS[2]
            elif offset == 1:
                maps[at, e, nodes] += -0.25 if slope else MASS[1]
            else:
                maps[at, e + 1, nodes] += -0.25 if slope else MASS[1]
    return maps


def unique_interp(elements):
    maps = np.zeros((8 * elements, elements + 1))
    for e in range(elements):
        maps[8 * e : 8 * e + 8, e] = INT[:, 0]
        maps[8 * e : 8 * e + 8, e + 1] = INT[:, 1]
    return maps


def unique_copies(elements):
    maps = np.zeros((2 * elements, elements + 1))
    for e in range(elements):
        maps[2 * e, e] = 1.0
        maps[2 * e + 1, e + 1] = 1.0
    return maps


def shifted(matrix):
    return np.stack(
        [np.array([matrix[a, (a - k) % 8] for a in range(8)]) for k in range(8)]
    )


def constants(ey, ez):
    parts = {}

    def spread(cols):
        return np.repeat(cols[..., None], 128, axis=-1)

    parts["grad_y"] = spread(shifted(DER)).reshape(64, 128)
    parts["back_y"] = spread(shifted(DER.T)).reshape(64, 128)
    parts["square_y"] = spread(shifted((DER * DER).T)).reshape(64, 128)
    parts["weight"] = WTS[:, None] * np.tile(WTS, 16)[None, :]
    order_z = (0, 1, -1)
    for name, slope in (("moment_m", False), ("moment_s", True)):
        block = np.zeros((128, 128))
        for at, one in enumerate(moment_maps(ez, order_z, slope)):
            block[:, 32 * at : 32 * at + ez + 1] = one.T
        parts[name] = block
    order_y = (-1, 0, 1)
    mass_y = np.zeros((3, 8, 8 * ey))
    mass_y[:, : ey + 1] = moment_maps(ey, order_y, False)
    slope_y = np.zeros((3, 8, 8 * ey))
    slope_y[:, : ey + 1] = moment_maps(ey, order_y, True)
    mass_y = mass_y.reshape(24, 8 * ey)
    slope_y = slope_y.reshape(24, 8 * ey)
    for name, sign in (("mix_plus", 0.25), ("mix_minus", -0.25)):
        block = np.zeros((24, 128))
        block[:, : 24 * ey] = np.concatenate([slope_y, mass_y, sign * mass_y], axis=1)
        parts[name] = block
    low = unique_interp(ey)
    block = np.zeros((16, 128))
    block[: ey + 1, : 8 * ey] = low.T
    block[8 : 8 + ey + 1, 8 * ey : 16 * ey] = low.T
    parts["rest_y"] = block
    block = np.zeros((128, 128))
    block[:, : ez + 1] = unique_interp(ez)
    parts["rest_z"] = block
    block = np.zeros((128, 128))
    block[: ez + 1, :] = unique_interp(ez).T
    parts["prol_z"] = block
    block = np.zeros((128, 128))
    block[: ez + 1, : 2 * ez] = unique_copies(ez).T
    parts["copy_z"] = block
    block = np.zeros((80, 128))
    for side in range(2):
        block[32 * side : 32 * side + 32, 8 * side : 8 * side + ey + 1] = low
        block[64 + 8 * side : 72 + 8 * side, 8 * side : 8 * side + ey + 1] = unique_copies(ey)
    parts["prol_y"] = block
    spots = {}
    at = 0
    for name, block in parts.items():
        spots[name] = (at, block.shape[0])
        at += block.shape[0]
    flat = np.concatenate(list(parts.values())).astype(np.float32)

    def halves(matrix):
        matrix = jnp.asarray(matrix, F32)
        high = matrix.astype(BF16)
        low = (matrix - high.astype(F32)).astype(BF16)
        top = jnp.concatenate([high, low], axis=1)
        return jnp.concatenate(
            [top, jnp.concatenate([high, jnp.zeros_like(low)], axis=1)], axis=0
        )

    eye = np.eye(ez)
    mats = jnp.stack(
        [halves(np.kron(eye, m)) for m in (DER.T, DER, DER * DER)]
    )
    return spots, jnp.asarray(flat), mats


def kernel(
    spots, n_dom, n_sub, coef_hbm, rhs_hbm, flat_hbm, mats_hbm, out_ref, coarse_ref,
    coef, rhs, flat, mats, weighted, field, held, fmask, fmult, inverse, pmine,
    xs1, ys1, es1, xs2, ys2, es2, ds, cs,
    xr1, yr1, er1, xr2, yr2, er2, pr, dr, cr,
    load_sem, s1, r1, sp, rp, sd, rd, s2, r2, s3, r3,
):
    dom = lax.axis_index("dom")
    sub = lax.axis_index("sub")

    def present(pair):
        dx, dy = pair
        conds = []
        if dx < 0:
            conds.append(dom >= -dx)
        if dx > 0:
            conds.append(dom < n_dom - dx)
        if dy < 0:
            conds.append(sub >= 1)
        if dy > 0:
            conds.append(sub < n_sub - 1)
        return functools.reduce(jnp.logical_and, conds)

    def target(pair):
        return (dom + pair[0], sub + pair[1])

    def piece(name):
        start, count = spots[name]
        return flat[start : start + count, :]

    for buffer in (xr1, yr1, er1, xr2, yr2, er2, pr, dr, cr):
        buffer[...] = jnp.zeros_like(buffer)

    barrier = pltpu.get_barrier_semaphore()
    for pair in WIDE:

        @pl.when(present(pair))
        def _(pair=pair):
            pl.semaphore_signal(barrier, inc=1, device_id=target(pair), device_id_type=MESH)

    loads = []
    for at, (source, dest) in enumerate(
        ((coef_hbm, coef), (flat_hbm, flat), (mats_hbm, mats), (rhs_hbm, rhs))
    ):
        load = pltpu.make_async_copy(source, dest, load_sem.at[at])
        load.start()
        loads.append(load)

    row = lax.broadcasted_iota(jnp.int32, (256, 128), 0)
    lane = lax.broadcasted_iota(jnp.int32, (256, 128), 1)
    x_at = lax.shift_right_logical(row, 5)
    y_at = row & 31
    place_x = dom * 8 + x_at
    place_y = sub * 32 + y_at
    inside = (
        (place_x > 0) & (place_x < 8 * n_dom - 1)
        & (place_y > 0) & (place_y < 32 * n_sub - 1)
        & (lane > 0) & (lane < 127)
    )
    mask = jnp.where(inside, 1.0, 0.0)
    fmask[...] = mask
    b_at = row & 7
    c_at = lane & 7
    twice = jnp.where((x_at == 0) | (x_at == 7), 2.0, 1.0)
    twice = twice * jnp.where((b_at == 0) | (b_at == 7), 2.0, 1.0)
    fmult[...] = mask * twice * jnp.where((c_at == 0) | (c_at == 7), 2.0, 1.0)

    lane8 = lax.broadcasted_iota(jnp.int32, (8, 128), 1)
    sub8 = lax.broadcasted_iota(jnp.int32, (8, 128), 0)
    z_low = ((lane8 & 7) == 0) & (lane8 > 0)
    z_high = ((lane8 & 7) == 7) & (lane8 < 127)

    def fold(v):
        v = v.reshape(32, 8, 128)
        v = v + jnp.where(
            z_high[None], pltpu.roll(v, 127, 2),
            jnp.where(z_low[None], pltpu.roll(v, 1, 2), 0.0),
        )
        v4 = v.reshape(8, 4, 8, 128)
        up = pltpu.roll(v, 1, 1).reshape(8, 4, 8, 128)
        down = pltpu.roll(v, 7, 1).reshape(8, 4, 8, 128)
        none = jnp.zeros((8, 1, 8, 128), F32)
        up = jnp.concatenate([none, up[:, :3]], axis=1)
        down = jnp.concatenate([down[:, 1:], none], axis=1)
        v4 = v4 + jnp.where(
            (sub8 == 0)[None, None], up, jnp.where((sub8 == 7)[None, None], down, 0.0)
        )
        return v4.reshape(256, 128)

    def along_x(v, matrix, sign):
        planes = v.reshape(8, 32, 128)
        even = [planes[b] + planes[7 - b] for b in range(4)]
        odd = [planes[b] - planes[7 - b] for b in range(4)]
        low = []
        high = []
        for a in range(4):
            p = sum(float(matrix[a, b] + matrix[a, 7 - b]) / 2 * even[b] for b in range(4))
            q = sum(float(matrix[a, b] - matrix[a, 7 - b]) / 2 * odd[b] for b in range(4))
            low.append(p + q)
            high.append(p - q if sign > 0 else q - p)
        return jnp.stack(low + high[::-1]).reshape(256, 128)

    def along_y(v, name):
        v = v.reshape(32, 8, 128)
        cols = piece(name).reshape(8, 8, 128)
        total = cols[0][None] * v
        for k in range(1, 8):
            total = total + cols[k][None] * pltpu.roll(v, k, 1)
        return total.reshape(256, 128)

    def along_z(v, at):
        high = v.astype(BF16)
        low = (v - high.astype(F32)).astype(BF16)
        both = jnp.concatenate([high, low], axis=1)
        wide = jnp.dot(both, mats[at], preferred_element_type=F32)
        return wide[:, :128] + wide[:, 128:]

    def local_operator(u):
        w = weighted[...]
        back = along_z(w * along_z(u, 0), 1)
        back = back + along_x(w * along_x(u, DER, -1), DER.T, -1)
        return back + along_y(w * along_y(u, "grad_y"), "back_y")

    def send(table, pair, source, landing, s_sem, r_sem):
        at = opposite(table, pair)

        @pl.when(present(pair))
        def _():
            pltpu.make_async_remote_copy(
                src_ref=source,
                dst_ref=landing.at[at],
                send_sem=s_sem.at[table.index(pair)],
                recv_sem=r_sem.at[at],
                device_id=target(pair),
                device_id_type=MESH,
            ).start()

    def settle(table, pair, source, landing, s_sem, r_sem, sent):
        at = table.index(pair)

        @pl.when(present(pair))
        def _():
            copy = pltpu.make_async_remote_copy(
                src_ref=source,
                dst_ref=landing.at[at],
                send_sem=s_sem.at[at],
                recv_sem=r_sem.at[at],
                device_id=target(pair),
                device_id_type=MESH,
            )
            if sent:
                copy.wait_send()
            else:
                copy.wait_recv()

    def corner_rows(low, high):
        tiles = {}
        for dx, dy in EDGE:
            face = low if dy < 0 else high
            keep = 0 if dx < 0 else 7
            goal = 7 if dx < 0 else 0
            tiles[(dx, dy)] = jnp.where(sub8 == goal, pltpu.roll(face, (goal - keep) % 8, 0), 0.0)
        return tiles

    def pack(refs, fields, xs, ys, es):
        for f in range(fields):
            ref = refs.at[f]
            low = ref[pl.ds(0, 8, stride=32), :]
            high = ref[pl.ds(31, 8, stride=32), :]
            xs[0, f] = ref[0:32, :]
            xs[1, f] = ref[224:256, :]
            ys[0, f] = low
            ys[1, f] = high
            tiles = corner_rows(low, high)
            for at, pair in enumerate(EDGE):
                es[at, f] = tiles[pair]

    def exchange(xs, ys, es, xr, yr, er, s_sem, r_sem):
        plan = []
        for pair in EDGE:
            plan.append((EDGE, pair, es.at[EDGE.index(pair)], er, s_sem.at[2], r_sem.at[2]))
        for pair in SIDE:
            plan.append((SIDE, pair, xs.at[SIDE.index(pair)], xr, s_sem.at[0], r_sem.at[0]))
        for pair in ROWS:
            plan.append((ROWS, pair, ys.at[ROWS.index(pair)], yr, s_sem.at[1], r_sem.at[1]))
        for item in plan:
            send(*item)
        return plan

    def unpack(refs, fields, xr, yr, er):
        for f in range(fields):
            ref = refs.at[f]
            ref[0:32, :] += xr[0, f]
            ref[224:256, :] += xr[1, f]
            for at, start in ((0, 0), (1, 31)):
                dy = ROWS[at][1]
                extra = yr[at, f]
                for number, pair in enumerate(EDGE):
                    if pair[1] == dy:
                        extra = extra + er[number, f]
                ref[pl.ds(start, 8, stride=32), :] += extra

    loads[0].wait()
    loads[1].wait()
    w_yz = piece("weight")
    planes = []
    c4 = coef[...].reshape(8, 4, 8, 128)
    for a in range(8):
        planes.append((c4[a] * (w_yz * float(WTS[a]))[None]).reshape(32, 128))
    w = jnp.concatenate(planes, axis=0)
    weighted[...] = w
    loads[2].wait()
    square = (DER * DER).T
    field[1] = fold(along_z(w, 2) + along_x(w, square, 1) + along_y(w, "square_y"))
    loads[3].wait()
    field[0] = fold(rhs[...].reshape(256, 128))
    pack(field, 2, xs1, ys1, es1)

    count_x = 1
    for offset in (1, 2):
        count_x = count_x + jnp.where(dom >= offset, 1, 0) + jnp.where(dom < n_dom - offset, 1, 0)
    count_y = 1 + jnp.where(sub >= 1, 1, 0) + jnp.where(sub < n_sub - 1, 1, 0)
    pl.semaphore_wait(barrier, count_x * count_y - 1)

    plans = exchange(xs1, ys1, es1, xr1, yr1, er1, s1, r1)
    first = list(plans)

    w3 = weighted[...].reshape(8, 32, 128)
    moments = [sum(float(m[a]) * w3[a] for a in range(8) if m[a] != 0.0) for m in MASS]
    moments.append(moments[0] + 2.0 * moments[1] + moments[2])
    stack = jnp.concatenate(moments, axis=0)
    mass_z = jnp.dot(stack, piece("moment_m"), precision=HIGHEST, preferred_element_type=F32)
    slope_z = jnp.dot(stack, piece("moment_s"), precision=HIGHEST, preferred_element_type=F32)
    none = jnp.zeros((32, 128), F32)
    for at in range(3):
        part = slice(32 * at, 32 * at + 32)
        parts = jnp.concatenate([mass_z[part], slope_z[part], mass_z[96:128], none], axis=0)
        mix = piece("mix_minus" if at == 1 else "mix_plus")
        pmine[at] = jnp.dot(mix, parts, precision=HIGHEST, preferred_element_type=F32)
    ds[0] = pmine[0, 8:16, :]
    ds[1] = pmine[2, 8:16, :]
    stencil = [(NEAR, pair, pmine, pr, sp, rp) for pair in NEAR]
    diags = [(FAR, pair, ds, dr, sd, rd) for pair in FAR]
    for item in stencil + diags:
        send(*item)

    for item in first:
        settle(*item, False)
    unpack(field, 2, xr1, yr1, er1)

    residual = fmask[...] * field[0]
    inv = fmask[...] / field[1]
    inverse[...] = inv
    field[0] = residual
    theta = 1.1
    delta = 0.9
    sigma = theta / delta
    rho0 = 1.0 / sigma
    rho1 = 1.0 / (2.0 * sigma - rho0)
    step_one = inv * residual / theta
    out_ref[...] = step_one.reshape(8, 32, 128)
    held[0] = fold(local_operator(step_one))
    pack(held, 1, xs2, ys2, es2)
    second_plan = exchange(xs2, ys2, es2, xr2, yr2, er2, s2, r2)

    for item in stencil + diags:
        settle(*item, False)

    def block(dx, dy, at):
        if (dx, dy) == (0, 0):
            return pmine[at]
        return pr[NEAR.index((dx, dy)), at]

    row_low = sub8 < 2
    row_mid = sub8 == 2

    def extend(parts):
        rows = []
        for v in range(4):
            sums = []
            for dy in (-1, 0, 1):
                one = parts(v - 2, dy, 1)
                two = parts(v - 1, dy, 0)
                sums.append(one + two)
            rim = jnp.where(row_low, sums[2], jnp.where(row_mid, 0.0, sums[0]))
            rows.append(pltpu.roll(sums[1], 1, 0) + pltpu.roll(rim, 5, 0))
        return rows

    def diag_part(dx, dy, vx):
        if abs(dx) == 2:
            return dr[FAR.index((dx, dy)), vx]
        return block(dx, dy, 2 * vx)[8:16]

    ext_diag = extend(diag_part)
    vertex_y = sub * 4 + sub8 - 1
    good_yz = (vertex_y > 0) & (vertex_y < 4 * n_sub) & (sub8 < 7) & (lane8 > 0) & (lane8 < 16)
    scales = []
    for v in range(4):
        vertex_x = dom + v - 1
        good = good_yz & (vertex_x > 0) & (vertex_x < n_dom)
        scales.append(jnp.where(good, (2.0 / 3.0) / jnp.where(good, ext_diag[v], 1.0), 0.0))

    row_is_0 = (sub8 == 0)[None]
    row_is_4 = (sub8 == 4)[None]
    joined = {}
    for dx in (-1, 0, 1):
        for at in range(3):
            rim = jnp.where(
                row_is_0, block(dx, 1, at).reshape(3, 8, 128),
                jnp.where(row_is_4, block(dx, -1, at).reshape(3, 8, 128), 0.0),
            )
            joined[(dx, at)] = block(dx, 0, at).reshape(3, 8, 128) + pltpu.roll(rim, 4, 1)
    stencils = [
        [joined[(-1, 1)], joined[(0, 0)] + joined[(-1, 2)], joined[(0, 1)]],
        [joined[(0, 1)], joined[(0, 2)] + joined[(1, 0)], joined[(1, 1)]],
    ]
    for vx in range(2):
        for at in range(3):
            mats_at = vx * 3 + at
            cs[1 + mats_at] = stencils[vx][at]

    for item in second_plan:
        settle(*item, False)
    unpack(held, 1, xr2, yr2, er2)
    residual = field[0]
    step_one = out_ref[...].reshape(256, 128)
    res_one = residual - fmask[...] * held[0]
    second = (1.0 + rho1 * rho0) * step_one + (2.0 * rho1 / delta) * inverse[...] * res_one
    out_ref[...] = second.reshape(8, 32, 128)

    defect = residual - fmult[...] * local_operator(second)
    d3 = defect.reshape(8, 32, 128)
    halves = jnp.concatenate(
        [sum(float(INT[a, i]) * d3[a] for a in range(8) if INT[a, i] != 0.0) for i in range(2)]
        + [jnp.zeros((64, 128), F32)],
        axis=0,
    )
    coarse = jnp.dot(piece("rest_y"), halves, precision=HIGHEST, preferred_element_type=F32)
    coarse = jnp.dot(coarse, piece("rest_z"), precision=HIGHEST, preferred_element_type=F32)
    cs[0, 0:2] = coarse.reshape(2, 8, 128)
    last = [(WIDE, pair, cs.at[0, pl.ds(0, 2)], cr, s3, r3) for pair in WIDE]
    for item in last:
        send(*item)
    for item in last:
        settle(*item, False)

    def rhs_part(dx, dy, vx):
        if (dx, dy) == (0, 0):
            return cs[0, vx]
        return cr[WIDE.index((dx, dy)), vx]

    ext_rhs = extend(rhs_part)
    ones = [scales[v] * ext_rhs[v] for v in range(4)]
    packed = [c + pltpu.roll(c, 31, 1) + pltpu.roll(c, 65, 1) for c in ones]
    around = [[c, pltpu.roll(c, 7, 0), pltpu.roll(c, 6, 0)] for c in packed]
    results = []
    for vx in range(2):
        total = jnp.zeros((8, 128), F32)
        for at in range(3):
            block3 = cs[1 + vx * 3 + at]
            for dy in range(3):
                total = total + block3[dy] * around[vx + at][dy]
        image = total + pltpu.roll(total, 96, 1) + pltpu.roll(total, 64, 1)
        one = pltpu.roll(ones[vx + 1], 7, 0)
        scale = pltpu.roll(scales[vx + 1], 7, 0)
        right = pltpu.roll(ext_rhs[vx + 1], 7, 0)
        results.append(one + scale * (right - image))
    both = jnp.concatenate(results, axis=0)
    nodes = jnp.dot(both, piece("prol_z"), precision=HIGHEST, preferred_element_type=F32)
    copies = jnp.dot(both, piece("copy_z"), precision=HIGHEST, preferred_element_type=F32)
    prol_y = piece("prol_y")[:, 0:16]
    fine = jnp.dot(prol_y[0:64], nodes, precision=HIGHEST, preferred_element_type=F32)
    copies = jnp.dot(prol_y[64:80], copies, precision=HIGHEST, preferred_element_type=F32)
    coarse_ref[...] = copies.reshape(2, 8, 128)[:, :, 0:32]
    for a in range(8):
        grown = float(INT[a, 0]) * fine[0:32] + float(INT[a, 1]) * fine[32:64]
        out_ref[a] = out_ref[a] + fmask[32 * a : 32 * a + 32, :] * grown

    for item in first + stencil + diags + second_plan + last:
        settle(*item, True)


def solution(mesh):
    n_dom = mesh.shape["dom"]
    n_sub = mesh.shape["sub"]

    def shards(rhs_local, coefficient):
        spots, flat, mats = constants(4, 16)
        any_space = pl.BlockSpec(memory_space=pl.ANY)
        vmem = pl.BlockSpec(memory_space=pltpu.VMEM)

        def space(*shape):
            return pltpu.VMEM(shape, F32)

        dma = pltpu.SemaphoreType.DMA
        return pl.pallas_call(
            functools.partial(kernel, spots, n_dom, n_sub),
            out_shape=(
                jax.ShapeDtypeStruct((8, 32, 128), F32),
                jax.ShapeDtypeStruct((2, 8, 32), F32),
            ),
            in_specs=[any_space] * 4,
            out_specs=(vmem, vmem),
            scratch_shapes=[
                space(8, 32, 128),
                space(8, 32, 128),
                pltpu.VMEM(flat.shape, F32),
                pltpu.VMEM(mats.shape, BF16),
                space(256, 128),
                space(2, 256, 128),
                space(1, 256, 128),
                space(256, 128),
                space(256, 128),
                space(256, 128),
                space(3, 24, 128),
                space(2, 2, 32, 128),
                space(2, 2, 8, 128),
                space(4, 2, 8, 128),
                space(2, 1, 32, 128),
                space(2, 1, 8, 128),
                space(4, 1, 8, 128),
                space(2, 8, 128),
                space(7, 3, 8, 128),
                space(2, 2, 32, 128),
                space(2, 2, 8, 128),
                space(4, 2, 8, 128),
                space(2, 1, 32, 128),
                space(2, 1, 8, 128),
                space(4, 1, 8, 128),
                space(8, 3, 24, 128),
                space(6, 2, 8, 128),
                space(14, 2, 8, 128),
                dma((4,)),
                dma((3, 4)),
                dma((3, 4)),
                dma((8,)),
                dma((8,)),
                dma((6,)),
                dma((6,)),
                dma((3, 4)),
                dma((3, 4)),
                dma((14,)),
                dma((14,)),
            ],
            compiler_params=pltpu.CompilerParams(collective_id=0, has_side_effects=True),
        )(coefficient, rhs_local, flat, mats)

    return jax.shard_map(
        shards,
        mesh=mesh,
        in_specs=(P("dom", "sub", None), P("dom", "sub", None)),
        out_specs=(P("dom", "sub", None), P("dom", "sub", None)),
        check_vma=False,
    )
```

time: 191 us -> 31.4 us (0.16)
  the two profiles are of different devices: /device:TPU:103 before, /device:TPU:1 now
where the time goes in v1:
time: 31.4 us; the launch traced here: 31.2 us
  Pallas kernels  28.4 us (90%)
  local copies, waits for them, and re-layouts  2.18 us (7%)
  between operations  0.65 us (2%)
    pallas_call x1, Pallas kernels, shards(): pl.pallas_call(functools.partial(kernel, spots, n_dom, n_sub), out_shape=...  28.4 us
    unnamed x4, local copies, waits for them, and re-layouts  2.18 us

profile of v1, /device:TPU:1, one launch (start us, length us, event | category | flops | bytes accessed | tf_op | source)
XLA Modules:
  0.0 31.2 jit_solution(1303436416869019154)
XLA Ops:
  0.6 28.4 %shard_map.77 = (f32[8,32,128]{2,1,0:T(8,128)}, f32[2,8,32]{2,1,0:T(8,128)}) custom-call(f32[8,32,128]{2,1,0:T(8,128)} %coef_hbm.1, f32[8,32,128]{2,1,0:T(8,128)} %rhs_hbm.1, f32[984,128]{1,0:T(8,128)} %constant.13.clone.flat_hbm, bf16[3,256,256]{2,1,0:T(8,128)(2,1)} %constant.46.mats_hbm), custom_call_target="tpu_custom_call" | custom-call | tf_op jit(solution)/shard_map/pallas_call | solution.py:567
  29.0 0.0 copy-start
  29.0 1.6 %copy.10 = f32[8,32,128]{2,1,0:T(8,128)} copy(f32[8,32,128]{2,1,0:T(8,128)} %get-tuple-element.4) | data formatting | bytes 262144
  30.6 0.0 copy-done
  30.6 0.6 %copy.11 = f32[2,8,32]{2,1,0:T(8,128)} copy(f32[2,8,32]{2,1,0:T(8,128)S(1)} %copy-done) | data formatting | bytes 4096
Async XLA Ops:
  29.0 1.6 %copy-start = (f32[2,8,32]{2,1,0:T(8,128)S(1)}, f32[2,8,32]{2,1,0:T(8,128)}, u32[]{:S(2)}) copy-start(f32[2,8,32]{2,1,0:T(8,128)} %get-tuple-element.5) | copy-start | bytes 6148

commit v2 on v1

v2 whole, which is shorter than its diff:
```python
import functools

import jax
import jax.numpy as jnp
import numpy as np
from jax import lax
from jax.experimental import pallas as pl
from jax.experimental.pallas import tpu as pltpu
from jax.sharding import PartitionSpec as P

MESH = pl.DeviceIdType.MESH
HIGHEST = lax.Precision.HIGHEST
F32 = jnp.float32
BF16 = jnp.bfloat16

NEAR = [(dx, dy) for dx in (-1, 0, 1) for dy in (-1, 0, 1) if (dx, dy) != (0, 0)]
WIDE = [(dx, dy) for dx in (-2, -1, 0, 1, 2) for dy in (-1, 0, 1) if (dx, dy) != (0, 0)]
SIDE = [pair for pair in NEAR if pair[1] == 0]
RIMS = [pair for pair in NEAR if pair[1] != 0]


def opposite(table, pair):
    return table.index((-pair[0], -pair[1]))


def tables():
    degree = 7
    points = np.array(
        [
            -1.0,
            -0.8717401485096066,
            -0.5917001814331423,
            -0.2092992179024789,
            0.2092992179024789,
            0.5917001814331423,
            0.8717401485096066,
            1.0,
        ]
    )
    previous = np.ones(points.shape)
    values = points.copy()
    for level in range(1, degree):
        following = ((2 * level + 1) * points * values - level * previous) / (level + 1)
        previous = values
        values = following
    weights = 2.0 / (degree * (degree + 1) * values**2)
    derivative = np.zeros((8, 8))
    for row_at in range(8):
        for col_at in range(8):
            if row_at != col_at:
                derivative[row_at, col_at] = values[row_at] / (
                    values[col_at] * (points[row_at] - points[col_at])
                )
    derivative[0, 0] = -degree * (degree + 1) / 4.0
    derivative[7, 7] = degree * (degree + 1) / 4.0
    interp = np.stack([(1.0 - points) / 2.0, (1.0 + points) / 2.0], axis=1)
    return derivative, weights, interp


DER, WTS, INT = tables()
MASS = [INT[:, 0] * INT[:, 0], INT[:, 0] * INT[:, 1], INT[:, 1] * INT[:, 1]]


def moment_maps(elements, order, slope):
    maps = np.zeros((len(order), elements + 1, 8 * elements))
    for at, offset in enumerate(order):
        for e in range(elements):
            nodes = slice(8 * e, 8 * e + 8)
            if offset == 0:
                maps[at, e, nodes] += 0.25 if slope else MASS[0]
                maps[at, e + 1, nodes] += 0.25 if slope else MASS[2]
            elif offset == 1:
                maps[at, e, nodes] += -0.25 if slope else MASS[1]
            else:
                maps[at, e + 1, nodes] += -0.25 if slope else MASS[1]
    return maps


def unique_interp(elements):
    maps = np.zeros((8 * elements, elements + 1))
    for e in range(elements):
        maps[8 * e : 8 * e + 8, e] = INT[:, 0]
        maps[8 * e : 8 * e + 8, e + 1] = INT[:, 1]
    return maps


def unique_copies(elements):
    maps = np.zeros((2 * elements, elements + 1))
    for e in range(elements):
        maps[2 * e, e] = 1.0
        maps[2 * e + 1, e + 1] = 1.0
    return maps


def split(matrix):
    high = jnp.asarray(matrix, F32).astype(BF16)
    return high, (jnp.asarray(matrix, F32) - high.astype(F32)).astype(BF16)


def right_halves(matrix):
    high, low = split(matrix)
    top = jnp.concatenate([high, low], axis=1)
    return jnp.concatenate([top, jnp.concatenate([high, jnp.zeros_like(low)], axis=1)], axis=0)


def left_halves(matrix):
    high, low = split(matrix)
    return jnp.concatenate([high, low, high, low], axis=1)


def wide(block):
    return jnp.pad(block, ((0, 0), (0, 256 - block.shape[1])))


def spots_of(parts):
    spots = {}
    at = 0
    for name, block in parts.items():
        spots[name] = (at, block.shape[0])
        at += block.shape[0]
    return spots, jnp.concatenate(list(parts.values()))


def constants(ey, ez):
    square = DER * DER
    eye8 = np.eye(8)
    eye = np.eye(ez)
    early = {
        "square_z": right_halves(np.kron(eye, square)),
        "square_xy": left_halves(np.kron(square.T, eye8) + np.kron(eye8, square.T)),
    }
    low = unique_interp(ey)
    place = np.zeros((4, 8, 8, 16))
    for side in range(2):
        place[..., 8 * side : 8 * side + ey + 1] = (
            INT[:, side][None, :, None, None] * low.reshape(ey, 8, ey + 1)[:, None]
        )
    place = place.reshape(256, 16)
    rest_z = np.zeros((128, 128))
    rest_z[:, : ez + 1] = unique_interp(ez)
    rest_z[:, 32 : 32 + ez + 1] = unique_interp(ez)
    prol_z = np.zeros((128, 128))
    prol_z[: ez + 1, :] = unique_interp(ez).T
    copy_z = np.zeros((128, 128))
    copy_z[: ez + 1, : 2 * ez] = unique_copies(ez).T
    copy_y = np.zeros((16, 16))
    for side in range(2):
        copy_y[8 * side : 8 * side + 8, 8 * side : 8 * side + ey + 1] = unique_copies(ey)
    rest_xy = split(place.T)
    late = {
        "grad_z": right_halves(np.kron(eye, DER.T)),
        "back_z": right_halves(np.kron(eye, DER)),
        "rest_z": right_halves(rest_z),
        "prol_z": right_halves(prol_z),
        "copy_z": wide(jnp.concatenate([split(copy_z)[0]] * 2)),
        "prol_xy": wide(left_halves(place)),
        "grad_xy": jnp.concatenate(
            [left_halves(np.kron(DER, eye8)), left_halves(np.kron(eye8, DER))]
        ),
        "back_x": left_halves(np.kron(DER.T, eye8)),
        "back_y": left_halves(np.kron(eye8, DER.T)),
        "rest_xy": jnp.concatenate([rest_xy[0], rest_xy[1]]),
        "copy_y": wide(left_halves(copy_y)),
    }
    flat = {}
    for name, slope in (("moment_m", False), ("moment_s", True)):
        block = np.zeros((128, 128))
        for at, one in enumerate(moment_maps(ez, (0, 1, -1), slope)):
            block[:, 32 * at : 32 * at + ez + 1] = one.T
        flat[name] = jnp.asarray(block, F32)
    order_y = (-1, 0, 1)
    mass_y = np.zeros((3, 8, 8 * ey))
    mass_y[:, : ey + 1] = moment_maps(ey, order_y, False)
    slope_y = np.zeros((3, 8, 8 * ey))
    slope_y[:, : ey + 1] = moment_maps(ey, order_y, True)
    mass_y = mass_y.reshape(24, 8 * ey)
    slope_y = slope_y.reshape(24, 8 * ey)
    for name, sign in (("mix_plus", 0.25), ("mix_minus", -0.25)):
        block = np.zeros((24, 128))
        block[:, : 24 * ey] = np.concatenate([slope_y, mass_y, sign * mass_y], axis=1)
        flat[name] = jnp.asarray(block, F32)
    return spots_of(early), spots_of(late), spots_of(flat)


def kernel(
    tables_at, n_dom, n_sub, coef_hbm, rhs_hbm, early_hbm, late_hbm, flat_hbm,
    out_ref, coarse_ref,
    coef, rhs, early, late, flat, weighted, field, held, fmask, fmult, inverse, step,
    pmine, ptile, dtile, ctile, stencil,
    xs1, vs1, xs2, vs2,
    xr1, vr1, xr2, vr2, px, pt, dr, cr,
    load_sem, s_sem, r_sem,
):
    early_at, late_at, flat_at = tables_at
    dom = lax.axis_index("dom")
    sub = lax.axis_index("sub")

    loads = []
    for at, (source, dest) in enumerate(
        ((coef_hbm, coef), (early_hbm, early), (rhs_hbm, rhs), (flat_hbm, flat), (late_hbm, late))
    ):
        load = pltpu.make_async_copy(source, dest, load_sem.at[at])
        load.start()
        loads.append(load)

    def present(pair):
        dx, dy = pair
        conds = []
        if dx < 0:
            conds.append(dom >= -dx)
        if dx > 0:
            conds.append(dom < n_dom - dx)
        if dy < 0:
            conds.append(sub >= 1)
        if dy > 0:
            conds.append(sub < n_sub - 1)
        return functools.reduce(jnp.logical_and, conds)

    def target(pair):
        return (dom + pair[0], sub + pair[1])

    for buffer in (xr1, vr1, xr2, vr2, px, pt, dr, cr):
        buffer[...] = jnp.zeros_like(buffer)

    barrier = pltpu.get_barrier_semaphore()
    for pair in WIDE:

        @pl.when(present(pair))
        def _(pair=pair):
            pl.semaphore_signal(barrier, inc=1, device_id=target(pair), device_id_type=MESH)

    near_x = jnp.where(dom >= 1, 1, 0) + jnp.where(dom < n_dom - 1, 1, 0)
    near_y = jnp.where(sub >= 1, 1, 0) + jnp.where(sub < n_sub - 1, 1, 0)
    far_x = near_x + jnp.where(dom >= 2, 1, 0) + jnp.where(dom < n_dom - 2, 1, 0)
    n_side = near_x
    n_rims = near_y * (1 + near_x)
    n_wide = (1 + far_x) * (1 + near_y) - 1

    row = lax.broadcasted_iota(jnp.int32, (256, 128), 0)
    lane = lax.broadcasted_iota(jnp.int32, (256, 128), 1)
    x_at = lax.shift_right_logical(row, 3) & 7
    b_at = row & 7
    c_at = lane & 7
    place_x = dom * 8 + x_at
    place_y = sub * 32 + lax.shift_right_logical(row, 6) * 8 + b_at
    inside = (
        (place_x > 0) & (place_x < 8 * n_dom - 1)
        & (place_y > 0) & (place_y < 32 * n_sub - 1)
        & (lane > 0) & (lane < 127)
    )
    mask = jnp.where(inside, 1.0, 0.0)
    fmask[...] = mask
    twice = jnp.where((x_at == 0) | (x_at == 7), 2.0, 1.0)
    twice = twice * jnp.where((b_at == 0) | (b_at == 7), 2.0, 1.0)
    fmult[...] = mask * twice * jnp.where((c_at == 0) | (c_at == 7), 2.0, 1.0)

    lane8 = lax.broadcasted_iota(jnp.int32, (8, 128), 1)
    sub8 = lax.broadcasted_iota(jnp.int32, (8, 128), 0)
    z_low = ((lane8 & 7) == 0) & (lane8 > 0)
    z_high = ((lane8 & 7) == 7) & (lane8 < 127)

    def weights_along(spot):
        value = jnp.where((spot == 0) | (spot == 7), float(WTS[0]), float(WTS[1]))
        value = jnp.where((spot == 2) | (spot == 5), float(WTS[2]), value)
        return jnp.where((spot == 3) | (spot == 4), float(WTS[3]), value)

    def fold(v):
        v = v.reshape(32, 8, 128)
        v = v + jnp.where(
            z_high[None], pltpu.roll(v, 127, 2),
            jnp.where(z_low[None], pltpu.roll(v, 1, 2), 0.0),
        )
        up = pltpu.roll(v, 1, 1)
        down = pltpu.roll(v, 7, 1)
        none = jnp.zeros((8, 8, 128), F32)
        up = jnp.concatenate([none, up[:24]], axis=0)
        down = jnp.concatenate([down[8:], none], axis=0)
        v = v + jnp.where((sub8 == 0)[None], up, jnp.where((sub8 == 7)[None], down, 0.0))
        return v.reshape(256, 128)

    def halves(v):
        high = v.astype(BF16)
        return high, (v - high.astype(F32)).astype(BF16)

    def dot(left, right):
        return jnp.dot(left, right, preferred_element_type=F32)

    def early_part(name):
        start, count = early_at[name]
        return early[start : start + count, :]

    def late_part(name):
        start, count = late_at[name]
        return late[start : start + count, :]

    def flat_part(name):
        start, count = flat_at[name]
        return flat[start : start + count, :]

    def times_right(pair, matrix):
        both = dot(jnp.concatenate(pair, axis=1), matrix)
        return both[:, :128] + both[:, 128:]

    def stacked(pair):
        high, low = [
            jnp.concatenate([v[64 * j : 64 * j + 64] for j in range(4)], axis=1) for v in pair
        ]
        return jnp.concatenate([high, high, low, low], axis=0)

    def rows_of(v):
        return jnp.concatenate([v[:, 128 * j : 128 * j + 128] for j in range(4)], axis=0)

    def local_operator(u):
        w = weighted[...]
        pair = halves(u)
        both = dot(late_part("grad_xy"), stacked(pair))
        flux_z = halves(w * times_right(pair, late_part("grad_z")))
        flux_x = halves(w * rows_of(both[0:64]))
        flux_y = halves(w * rows_of(both[64:128]))
        back = dot(late_part("back_x"), stacked(flux_x))
        back = back + dot(late_part("back_y"), stacked(flux_y))
        return rows_of(back) + times_right(flux_z, late_part("back_z"))

    def send(table, pair, source, landing, group):
        at = table.index((-pair[0], -pair[1]))

        @pl.when(present(pair))
        def _():
            pltpu.make_async_remote_copy(
                src_ref=source,
                dst_ref=landing.at[at],
                send_sem=s_sem.at[group],
                recv_sem=r_sem.at[group],
                device_id=target(pair),
                device_id_type=MESH,
            ).start()

    counts = {"side": (n_side, (1, 2)), "rims": (n_rims, (1, 2, 3, 4, 6)), "wide": (n_wide, (1, 2, 3, 5, 7, 8, 9, 11, 14))}

    def settle(kind, landing, group, sent):
        count, options = counts[kind]
        for one in options:

            @pl.when(count == one)
            def _(one=one):
                copy = pltpu.make_async_remote_copy(
                    src_ref=landing.at[pl.ds(0, one)],
                    dst_ref=landing.at[pl.ds(0, one)],
                    send_sem=s_sem.at[group],
                    recv_sem=r_sem.at[group],
                    device_id=(dom, sub),
                    device_id_type=MESH,
                )
                if sent:
                    copy.wait_send()
                else:
                    copy.wait_recv()

    def pack(refs, fields, xs, vs):
        for f in range(fields):
            ref = refs.at[f]
            faces = {-1: ref[pl.ds(0, 8, stride=8), :], 1: ref[pl.ds(199, 8, stride=8), :]}
            for j in range(4):
                xs[0, f, 8 * j : 8 * j + 8] = ref[64 * j : 64 * j + 8, :]
                xs[1, f, 8 * j : 8 * j + 8] = ref[64 * j + 56 : 64 * j + 64, :]
            for at, (dx, dy) in enumerate(RIMS):
                face = faces[dy]
                if dx < 0:
                    face = jnp.where(sub8 == 7, pltpu.roll(face, 7, 0), 0.0)
                if dx > 0:
                    face = jnp.where(sub8 == 0, pltpu.roll(face, 1, 0), 0.0)
                vs[at, f] = face

    def exchange(xs, vs, xr, vr, group):
        for pair in RIMS:
            if pair[0] != 0:
                send(RIMS, pair, vs.at[RIMS.index(pair)], vr, group + 1)
        for pair in SIDE:
            send(SIDE, pair, xs.at[SIDE.index(pair)], xr, group)
        for pair in RIMS:
            if pair[0] == 0:
                send(RIMS, pair, vs.at[RIMS.index(pair)], vr, group + 1)

    def unpack(refs, fields, xr, vr):
        for f in range(fields):
            ref = refs.at[f]
            for j in range(4):
                ref[64 * j : 64 * j + 8, :] += xr[0, f, 8 * j : 8 * j + 8]
                ref[64 * j + 56 : 64 * j + 64, :] += xr[1, f, 8 * j : 8 * j + 8]
            for dy, start in ((-1, 0), (1, 199)):
                a, b, c = [vr[RIMS.index((dx, dy)), f] for dx in (-1, 0, 1)]
                ref[pl.ds(start, 8, stride=8), :] += a + b + c

    def in_order(ref):
        v = ref[...].reshape(8, 4, 8, 128)
        return jnp.concatenate([v[:, j] for j in range(4)], axis=0).reshape(256, 128)

    table = weights_along(x_at) * weights_along(b_at) * weights_along(c_at)
    loads[0].wait()
    w = in_order(coef) * table
    weighted[...] = w
    loads[1].wait()
    pair = halves(w)
    diagonal = rows_of(dot(early_part("square_xy"), stacked(pair)))
    field[1] = fold(diagonal + times_right(pair, early_part("square_z")))
    loads[2].wait()
    field[0] = fold(in_order(rhs))
    pack(field, 2, xs1, vs1)

    pl.semaphore_wait(barrier, n_wide)
    exchange(xs1, vs1, xr1, vr1, 0)

    loads[3].wait()
    w4 = weighted[...].reshape(4, 8, 8, 128)
    planes = [w4[:, a].reshape(32, 128) for a in range(8)]
    moments = [sum(float(m[a]) * planes[a] for a in range(8) if m[a] != 0.0) for m in MASS]
    moments.append(moments[0] + 2.0 * moments[1] + moments[2])
    stack = jnp.concatenate(moments, axis=0)
    mass_z = jnp.dot(stack, flat_part("moment_m"), precision=HIGHEST, preferred_element_type=F32)
    slope_z = jnp.dot(stack, flat_part("moment_s"), precision=HIGHEST, preferred_element_type=F32)
    none = jnp.zeros((32, 128), F32)
    mine = []
    for at in range(3):
        part = slice(32 * at, 32 * at + 32)
        parts = jnp.concatenate([mass_z[part], slope_z[part], mass_z[96:128], none], axis=0)
        mix = flat_part("mix_minus" if at == 1 else "mix_plus")
        one = jnp.dot(mix, parts, precision=HIGHEST, preferred_element_type=F32)
        pmine[at] = one
        mine.append(one.reshape(3, 8, 128))
    dtile[...] = jnp.where(lane8 < 32, mine[0][1], pltpu.roll(mine[2][1], 32, 1))
    for tile, vertex, first in ((0, 0, 1), (1, 4, 0)):
        total = jnp.zeros((8, 128), F32)
        for c in range(3):
            for d in range(2):
                goal = 2 * c + d
                moved = pltpu.roll(mine[c][first + d], (goal - vertex) % 8, 0)
                total = jnp.where(sub8 == goal, moved, total)
        ptile[tile] = total
    send(SIDE, (-1, 0), pmine.at[pl.ds(0, 2)], px, 2)
    send(SIDE, (1, 0), pmine.at[pl.ds(1, 2)], px, 2)
    for pair in RIMS:
        send(RIMS, pair, ptile.at[0 if pair[1] < 0 else 1], pt, 3)
    for pair in WIDE:
        send(WIDE, pair, dtile, dr, 4)
    loads[4].wait()

    settle("side", xr1, 0, False)
    settle("rims", vr1, 1, False)
    unpack(field, 2, xr1, vr1)

    residual = fmask[...] * field[0]
    inv = fmask[...] / field[1]
    inverse[...] = inv
    field[0] = residual
    theta = 1.1
    delta = 0.9
    sigma = theta / delta
    rho0 = 1.0 / sigma
    rho1 = 1.0 / (2.0 * sigma - rho0)
    step_one = inv * residual / theta
    step[...] = step_one
    held[0] = fold(local_operator(step_one))
    pack(held, 1, xs2, vs2)
    exchange(xs2, vs2, xr2, vr2, 5)

    settle("side", px, 2, False)
    settle("rims", pt, 3, False)
    settle("wide", dr, 4, False)

    row_low = sub8 < 2
    row_mid = sub8 == 2

    def extend(own, received):
        moved = []
        for dx in (-2, -1, 0, 1, 2):
            mid = own if dx == 0 else received[WIDE.index((dx, 0))]
            below = received[WIDE.index((dx, -1))]
            above = received[WIDE.index((dx, 1))]
            rim = jnp.where(row_low, above, jnp.where(row_mid, 0.0, below))
            moved.append(pltpu.roll(mid, 1, 0) + pltpu.roll(rim, 5, 0))
        return [moved[v + 1] + pltpu.roll(moved[v], 96, 1) for v in range(4)]

    ext_diag = extend(dtile[...], dr)
    vertex_y = sub * 4 + sub8 - 1
    good_yz = (vertex_y > 0) & (vertex_y < 4 * n_sub) & (sub8 < 7) & (lane8 > 0) & (lane8 < 16)
    scales = []
    for v in range(4):
        vertex_x = dom + v - 1
        good = good_yz & (vertex_x > 0) & (vertex_x < n_dom)
        scales.append(jnp.where(good, (2.0 / 3.0) / jnp.where(good, ext_diag[v], 1.0), 0.0))

    def joined(dx, c):
        if dx == 0:
            base = pmine[c]
        else:
            base = px[SIDE.index((dx, 0)), c if dx > 0 else c - 1]
        base = base.reshape(3, 8, 128)
        below = pt[RIMS.index((dx, -1))]
        above = pt[RIMS.index((dx, 1))]
        out = []
        for d in range(3):
            total = base[d]
            if d < 2:
                moved = pltpu.roll(below, (-2 * c - d) % 8, 0)
                total = total + jnp.where(sub8 == 0, moved, 0.0)
            if d > 0:
                moved = pltpu.roll(above, (4 - 2 * c - (d - 1)) % 8, 0)
                total = total + jnp.where(sub8 == 4, moved, 0.0)
            out.append(total)
        return out

    cross = joined(0, 1)
    own_low = [a + b for a, b in zip(joined(0, 0), joined(-1, 2), strict=True)]
    own_high = [a + b for a, b in zip(joined(0, 2), joined(1, 0), strict=True)]
    for vx, blocks in enumerate(
        ((joined(-1, 1), own_low, cross), (cross, own_high, joined(1, 1)))
    ):
        for at in range(3):
            for d in range(3):
                stencil[vx * 9 + at * 3 + d] = blocks[at][d]
    for v in range(4):
        stencil[18 + v] = scales[v]

    settle("side", xr2, 5, False)
    settle("rims", vr2, 6, False)
    unpack(held, 1, xr2, vr2)
    residual = field[0]
    step_one = step[...]
    res_one = residual - fmask[...] * held[0]
    second = (1.0 + rho1 * rho0) * step_one + (2.0 * rho1 / delta) * inverse[...] * res_one
    step[...] = second

    defect = residual - fmult[...] * local_operator(second)
    part = dot(late_part("rest_xy"), jnp.concatenate(halves(defect), axis=1))
    part = part[0:16, :128] + part[0:16, 128:] + part[16:32, :128]
    coarse = times_right(halves(part), late_part("rest_z"))
    ctile[...] = jnp.where(lane8 < 32, coarse[0:8], coarse[8:16])
    for pair in sorted(WIDE, key=lambda p: -abs(p[0]) - abs(p[1])):
        send(WIDE, pair, ctile, cr, 7)

    settle("side", xr1, 0, True)
    settle("rims", vr1, 1, True)
    settle("side", px, 2, True)
    settle("rims", pt, 3, True)
    settle("wide", dr, 4, True)
    settle("side", xr2, 5, True)
    settle("rims", vr2, 6, True)
    settle("wide", cr, 7, False)

    ext_rhs = extend(ctile[...], cr)
    scales = [stencil[18 + v] for v in range(4)]
    ones = [scales[v] * ext_rhs[v] for v in range(4)]
    packed = [c + pltpu.roll(c, 31, 1) + pltpu.roll(c, 65, 1) for c in ones]
    around = [[c, pltpu.roll(c, 7, 0), pltpu.roll(c, 6, 0)] for c in packed]
    results = []
    for vx in range(2):
        total = jnp.zeros((8, 128), F32)
        for at in range(3):
            for d in range(3):
                total = total + stencil[vx * 9 + at * 3 + d] * around[vx + at][d]
        image = total + pltpu.roll(total, 96, 1) + pltpu.roll(total, 64, 1)
        one = pltpu.roll(ones[vx + 1], 7, 0)
        scale = pltpu.roll(scales[vx + 1], 7, 0)
        right = pltpu.roll(ext_rhs[vx + 1], 7, 0)
        results.append(one + scale * (right - image))
    pair = halves(jnp.concatenate(results, axis=0))
    nodes = halves(times_right(pair, late_part("prol_z")))
    nodes = jnp.concatenate([nodes[0], nodes[0], nodes[1], nodes[1]], axis=0)
    fine = step[...] + fmask[...] * dot(late_part("prol_xy")[:, 0:64], nodes)
    fine = fine.reshape(4, 8, 8, 128)
    for j in range(4):
        out_ref[:, 8 * j : 8 * j + 8, :] = fine[j]
    copies = halves(dot(jnp.concatenate(pair, axis=1), late_part("copy_z")[:, 0:128]))
    copies = jnp.concatenate([copies[0], copies[0], copies[1], copies[1]], axis=0)
    copies = dot(late_part("copy_y")[:, 0:64], copies)
    coarse_ref[...] = copies.reshape(2, 8, 128)[:, :, 0:32]

    settle("wide", cr, 7, True)


def finish(fine, coarse, fine_out, coarse_out, sem):
    one = pltpu.make_async_copy(fine, fine_out, sem.at[0])
    two = pltpu.make_async_copy(coarse, coarse_out, sem.at[1])
    one.start()
    two.start()
    one.wait()
    two.wait()


def solution(mesh):
    n_dom = mesh.shape["dom"]
    n_sub = mesh.shape["sub"]

    def shards(rhs_local, coefficient):
        (early_at, early), (late_at, late), (flat_at, flat) = constants(4, 16)
        any_space = pl.BlockSpec(memory_space=pl.ANY)
        vmem = pl.BlockSpec(memory_space=pltpu.VMEM)
        outs = (
            jax.ShapeDtypeStruct((8, 32, 128), F32),
            jax.ShapeDtypeStruct((2, 8, 32), F32),
        )

        def space(*shape):
            return pltpu.VMEM(shape, F32)

        dma = pltpu.SemaphoreType.DMA
        operands = [
            pltpu.with_memory_space_constraint(v, pltpu.HBM)
            for v in (coefficient, rhs_local, early, late, flat)
        ]
        fine, coarse = pl.pallas_call(
            functools.partial(kernel, (early_at, late_at, flat_at), n_dom, n_sub),
            out_shape=outs,
            in_specs=[any_space] * 5,
            out_specs=(vmem, vmem),
            scratch_shapes=[
                space(8, 32, 128),
                space(8, 32, 128),
                pltpu.VMEM(early.shape, BF16),
                pltpu.VMEM(late.shape, BF16),
                pltpu.VMEM(flat.shape, F32),
                space(256, 128),
                space(2, 256, 128),
                space(1, 256, 128),
                space(256, 128),
                space(256, 128),
                space(256, 128),
                space(256, 128),
                space(3, 24, 128),
                space(2, 8, 128),
                space(8, 128),
                space(8, 128),
                space(22, 8, 128),
                space(2, 2, 32, 128),
                space(6, 2, 8, 128),
                space(2, 1, 32, 128),
                space(6, 1, 8, 128),
                space(2, 2, 32, 128),
                space(6, 2, 8, 128),
                space(2, 1, 32, 128),
                space(6, 1, 8, 128),
                space(2, 2, 24, 128),
                space(6, 8, 128),
                space(14, 8, 128),
                space(14, 8, 128),
                dma((5,)),
                dma((8,)),
                dma((8,)),
            ],
            compiler_params=pltpu.CompilerParams(
                collective_id=0, has_side_effects=True, vmem_limit_bytes=8 * 2**20
            ),
        )(*operands)
        return pl.pallas_call(
            finish,
            out_shape=outs,
            in_specs=[vmem, vmem],
            out_specs=(any_space, any_space),
            scratch_shapes=[dma((2,))],
            compiler_params=pltpu.CompilerParams(vmem_limit_bytes=2**20),
        )(fine, coarse)

    return jax.shard_map(
        shards,
        mesh=mesh,
        in_specs=(P("dom", "sub", None), P("dom", "sub", None)),
        out_specs=(P("dom", "sub", None), P("dom", "sub", None)),
        check_vma=False,
    )
```

time: 31.4 us -> 28.1 us (0.89)
  local copies, waits for them, and re-layouts: 2.18 us -> 0 us
  Pallas kernels: 28.4 us -> 27.3 us
    unnamed x4 -> x0, local copies, waits for them, and re-layouts: 2.18 us -> none
    pallas_call x1 -> x2, Pallas kernels: 28.4 us -> 27.3 us  [the longest x1 26.6 us: shards(): pl.pallas_call(functools.partial(kernel, (early_at, late_at, flat_at), n_...]
where the time goes in v2:
time: 28.1 us; the launch traced here: 28 us
  Pallas kernels  27.3 us (97%)
  between operations  0.64 us (2%)
    pallas_call x1, Pallas kernels, shards(): pl.pallas_call(functools.partial(kernel, (early_at, late_at, flat_at), n_...  26.6 us
    pallas_call x1, Pallas kernels, shards(): pl.pallas_call(finish, out_shape=outs, in_specs=[vmem, vmem], out_specs=(...  0.68 us

profile of v2, /device:TPU:1, one launch (start us, length us, event | category | flops | bytes accessed | tf_op | source)
XLA Modules:
  0.0 28.0 jit_solution(2440395745828120176)
XLA Ops:
  0.6 26.6 %shard_map.320 = (f32[8,32,128]{2,1,0:T(8,128)S(1)}, f32[2,8,32]{2,1,0:T(8,128)S(1)}) custom-call(f32[8,32,128]{2,1,0:T(8,128)} %coef_hbm.1, f32[8,32,128]{2,1,0:T(8,128)} %rhs_hbm.1, bf16[320,256]{1,0:T(8,128)(2,1)} %constant.87.early_hbm, bf16[1840,256]{1,0:T(8,128)(2,1)} %constant.151.late_hbm, f32[304,128]{1,0:T(8,128)} %constant.152.flat_hbm), custom_call_target="tpu_custom_call" | custom-call | tf_op jit(solution)/shard_map/pallas_call | solution.py:611
  27.3 0.7 %shard_map.321 = (f32[8,32,128]{2,1,0:T(8,128)}, f32[2,8,32]{2,1,0:T(8,128)}) custom-call(f32[8,32,128]{2,1,0:T(8,128)S(1)} %get-tuple-element.4.fine, f32[2,8,32]{2,1,0:T(8,128)S(1)} %get-tuple-element.5.coarse), custom_call_target="tpu_custom_call" | custom-call | tf_op jit(solution)/shard_map/pallas_call | solution.py:654

commit v3 on v2

--- a/solution.py
+++ b/solution.py
@@ -15,8 +15,11 @@
 
 NEAR = [(dx, dy) for dx in (-1, 0, 1) for dy in (-1, 0, 1) if (dx, dy) != (0, 0)]
 WIDE = [(dx, dy) for dx in (-2, -1, 0, 1, 2) for dy in (-1, 0, 1) if (dx, dy) != (0, 0)]
+REACH = [(dx, dy) for dx in range(-3, 4) for dy in (-1, 0, 1) if (dx, dy) != (0, 0)]
 SIDE = [pair for pair in NEAR if pair[1] == 0]
 RIMS = [pair for pair in NEAR if pair[1] != 0]
+EDGE = [pair for pair in RIMS if pair[0] != 0]
+ROWS = [pair for pair in RIMS if pair[0] == 0]
 
 
 def opposite(table, pair):
@@ -58,6 +61,13 @@
 
 
 DER, WTS, INT = tables()
+TWICE = np.array([2.0, 1.0, 1.0, 1.0, 1.0, 1.0, 1.0, 2.0])
+HATS = [TWICE * INT[:, 0], TWICE * INT[:, 1]]
+
+
+def face_moments(face):
+    near = 0 if face == 0 else 1
+    return [DER[:, face] * (DER @ HATS[i]) for i in (near, 1 - near)]
 MASS = [INT[:, 0] * INT[:, 0], INT[:, 0] * INT[:, 1], INT[:, 1] * INT[:, 1]]
 
 
@@ -105,7 +115,7 @@
 
 def left_halves(matrix):
     high, low = split(matrix)
-    return jnp.concatenate([high, low, high, low], axis=1)
+    return jnp.concatenate([high, low, high], axis=1)
 
 
 def wide(block):
@@ -127,7 +137,7 @@
     eye = np.eye(ez)
     early = {
         "square_z": right_halves(np.kron(eye, square)),
-        "square_xy": left_halves(np.kron(square.T, eye8) + np.kron(eye8, square.T)),
+        "square_xy": wide(left_halves(np.kron(square.T, eye8) + np.kron(eye8, square.T))),
     }
     low = unique_interp(ey)
     place = np.zeros((4, 8, 8, 16))
@@ -138,7 +148,8 @@
     place = place.reshape(256, 16)
     rest_z = np.zeros((128, 128))
     rest_z[:, : ez + 1] = unique_interp(ez)
-    rest_z[:, 32 : 32 + ez + 1] = unique_interp(ez)
+    for at in (32, 64, 96):
+        rest_z[:, at : at + ez + 1] = unique_interp(ez)
     prol_z = np.zeros((128, 128))
     prol_z[: ez + 1, :] = unique_interp(ez).T
     copy_z = np.zeros((128, 128))
@@ -146,7 +157,60 @@
     copy_y = np.zeros((16, 16))
     for side in range(2):
         copy_y[8 * side : 8 * side + 8, 8 * side : 8 * side + ey + 1] = unique_copies(ey)
-    rest_xy = split(place.T)
+    own = np.zeros((32, 256))
+    for side in range(2):
+        own[8 * (side + 1) + 1 : 8 * (side + 1) + 2 + ey] = place.T[8 * side : 8 * side + ey + 1]
+    rest_xy = split(own)
+    spill = np.zeros((4, 8, 256))
+    low_m = low * np.tile(TWICE, ey)[:, None]
+    for side in range(2):
+        for at, v in ((0, 1 + side), (64, 3 * side)):
+            spill[v, 1 : ey + 2, at + 32 * side : at + 32 * side + 32] = low_m.T
+        for at, r in ((128, 1 + ey * side), (144, (ey + 2) * side)):
+            for vx in range(2):
+                spill[1 + vx, r, at + 8 * side : at + 8 * side + 8] = HATS[vx]
+    for at, (dx, dy) in enumerate(EDGE):
+        near_v, far_v = (1, 0) if dx < 0 else (2, 3)
+        near_r, far_r = (1, 0) if dy < 0 else (1 + ey, 2 + ey)
+        spill[near_v, near_r, 160 + at] = 1.0
+        spill[far_v, near_r, 168 + at] = 1.0
+        spill[near_v, far_r, 176 + at] = 1.0
+    spill = split(spill.reshape(32, 256))
+    rest_z = np.zeros((128, 128))
+    rest_z[:, : ez + 1] = unique_interp(ez)
+    for at in (32, 64, 96):
+        rest_z[:, at : at + ez + 1] = unique_interp(ez)
+    prol_z = np.zeros((128, 128))
+    prol_z[: ez + 1, :] = unique_interp(ez).T
+    copy_z = np.zeros((128, 128))
+    copy_z[: ez + 1, : 2 * ez] = unique_copies(ez).T
+    copy_y = np.zeros((16, 16))
+    for side in range(2):
+        copy_y[8 * side : 8 * side + 8, 8 * side : 8 * side + ey + 1] = unique_copies(ey)
+    own = np.zeros((32, 256))
+    for side in range(2):
+        own[8 * (side + 1) + 1 : 8 * (side + 1) + 2 + ey] = place.T[8 * side : 8 * side + ey + 1]
+    rest_xy = split(own)
+    spill = np.zeros((4, 8, 256))
+    low_m = low * np.tile(TWICE, ey)[:, None]
+    for side in range(2):
+        for at, v in ((0, 1 + side), (64, 3 * side)):
+            spill[v, 1 : ey + 2, at + 32 * side : at + 32 * side + 32] = low_m.T
+        for at, r in ((128, 1 + ey * side), (144, (ey + 2) * side)):
+            for vx in range(2):
+                spill[1 + vx, r, at + 8 * side : at + 8 * side + 8] = HATS[vx]
+    for at, (dx, dy) in enumerate(EDGE):
+        near_v, far_v = (1, 0) if dx < 0 else (2, 3)
+        near_r, far_r = (1, 0) if dy < 0 else (1 + ey, 2 + ey)
+        spill[near_v, near_r, 160 + at] = 1.0
+        spill[far_v, near_r, 168 + at] = 1.0
+        spill[near_v, far_r, 176 + at] = 1.0
+    spill = split(spill.reshape(32, 256))
+    moment_y = np.zeros((2, 2, 8, 8, 8))
+    for side in range(2):
+        for at, one in enumerate(face_moments(7 * side)):
+            moment_y[side, at] = np.eye(8)[:, :, None] * one[None, None, :]
+    moment_y = moment_y.reshape(32, 64)
     late = {
         "grad_z": right_halves(np.kron(eye, DER.T)),
         "back_z": right_halves(np.kron(eye, DER)),
@@ -154,12 +218,12 @@
         "prol_z": right_halves(prol_z),
         "copy_z": wide(jnp.concatenate([split(copy_z)[0]] * 2)),
         "prol_xy": wide(left_halves(place)),
-        "grad_xy": jnp.concatenate(
-            [left_halves(np.kron(DER, eye8)), left_halves(np.kron(eye8, DER))]
+        "grad_xy": wide(
+            jnp.concatenate([left_halves(np.kron(DER, eye8)), left_halves(np.kron(eye8, DER))])
         ),
-        "back_x": left_halves(np.kron(DER.T, eye8)),
-        "back_y": left_halves(np.kron(eye8, DER.T)),
+        "back_y": wide(left_halves(np.kron(eye8, DER.T))),
         "rest_xy": jnp.concatenate([rest_xy[0], rest_xy[1]]),
+        "spill": jnp.concatenate([spill[0], spill[1]]),
         "copy_y": wide(left_halves(copy_y)),
     }
     flat = {}
@@ -186,9 +250,9 @@
     tables_at, n_dom, n_sub, coef_hbm, rhs_hbm, early_hbm, late_hbm, flat_hbm,
     out_ref, coarse_ref,
     coef, rhs, early, late, flat, weighted, field, held, fmask, fmult, inverse, step,
-    pmine, ptile, dtile, ctile, stencil,
+    pmine, ptile, dtile, ctile, stencil, gfield, fside, frow, fedge,
     xs1, vs1, xs2, vs2,
-    xr1, vr1, xr2, vr2, px, pt, dr, cr,
+    xr1, vr1, xr2, vr2, px, pt, dr, cr, fx, fy, fe,
     load_sem, s_sem, r_sem,
 ):
     early_at, late_at, flat_at = tables_at
@@ -219,11 +283,11 @@
     def target(pair):
         return (dom + pair[0], sub + pair[1])
 
-    for buffer in (xr1, vr1, xr2, vr2, px, pt, dr, cr):
+    for buffer in (xr1, vr1, xr2, vr2, px, pt, dr, cr, fx, fy, fe):
         buffer[...] = jnp.zeros_like(buffer)
 
     barrier = pltpu.get_barrier_semaphore()
-    for pair in WIDE:
+    for pair in sorted(REACH, key=lambda p: abs(p[0]) + abs(p[1])):
 
         @pl.when(present(pair))
         def _(pair=pair):
@@ -235,6 +299,8 @@
     n_side = near_x
     n_rims = near_y * (1 + near_x)
     n_wide = (1 + far_x) * (1 + near_y) - 1
+    reach_x = far_x + jnp.where(dom >= 3, 1, 0) + jnp.where(dom < n_dom - 3, 1, 0)
+    n_reach = (1 + reach_x) * (1 + near_y) - 1
 
     row = lax.broadcasted_iota(jnp.int32, (256, 128), 0)
     lane = lax.broadcasted_iota(jnp.int32, (256, 128), 1)
@@ -303,23 +369,47 @@
 
     def stacked(pair):
         high, low = [
-            jnp.concatenate([v[64 * j : 64 * j + 64] for j in range(4)], axis=1) for v in pair
+            jnp.concatenate([v[at : at + 64] for at in range(0, v.shape[0], 64)], axis=1) for v in pair
         ]
-        return jnp.concatenate([high, high, low, low], axis=0)
+        return jnp.concatenate([high, high, low], axis=0)
 
     def rows_of(v):
-        return jnp.concatenate([v[:, 128 * j : 128 * j + 128] for j in range(4)], axis=0)
+        return jnp.concatenate([v[:, at : at + 128] for at in range(0, v.shape[1], 128)], axis=0)
+
+    def back_x(v):
+        v = v.reshape(4, 8, 8, 128)
+        matrix = DER.T
+        even = [v[:, b] + v[:, 7 - b] for b in range(4)]
+        odd = [v[:, b] - v[:, 7 - b] for b in range(4)]
+        planes = [None] * 8
+        for a in range(4):
+            p = sum(float(matrix[a, b] + matrix[a, 7 - b]) / 2 * even[b] for b in range(4))
+            q = sum(float(matrix[a, b] - matrix[a, 7 - b]) / 2 * odd[b] for b in range(4))
+            planes[a] = p + q
+            planes[7 - a] = q - p
+        return jnp.stack(planes, axis=1).reshape(256, 128)
+
+    def with_faces(u, faces, w_rows, w_z):
+        w = weighted[...]
+        pair = halves(jnp.concatenate([u, faces], axis=0))
+        both = dot(late_part("grad_xy")[:, 0:192], stacked(pair))
+        all_z = times_right(pair, late_part("grad_z"))
+        all_y = rows_of(both[64:128])
+        flux_z = halves(jnp.concatenate([w * all_z[0:256], w_z * all_z[256:384]], axis=0))
+        flux_y = halves(jnp.concatenate([w * all_y[0:256], w_rows * all_y[256:384]], axis=0))
+        back = rows_of(dot(late_part("back_y")[:, 0:192], stacked(flux_y)))
+        back = back + times_right(flux_z, late_part("back_z"))
+        return back[0:256] + back_x(w * rows_of(both[0:64, 0:512])), back[256:384]
 
     def local_operator(u):
         w = weighted[...]
         pair = halves(u)
-        both = dot(late_part("grad_xy"), stacked(pair))
+        both = dot(late_part("grad_xy")[:, 0:192], stacked(pair))
         flux_z = halves(w * times_right(pair, late_part("grad_z")))
-        flux_x = halves(w * rows_of(both[0:64]))
         flux_y = halves(w * rows_of(both[64:128]))
-        back = dot(late_part("back_x"), stacked(flux_x))
-        back = back + dot(late_part("back_y"), stacked(flux_y))
-        return rows_of(back) + times_right(flux_z, late_part("back_z"))
+        back = rows_of(dot(late_part("back_y")[:, 0:192], stacked(flux_y)))
+        back = back + times_right(flux_z, late_part("back_z"))
+        return back + back_x(w * rows_of(both[0:64]))
 
     def send(table, pair, source, landing, group):
         at = table.index((-pair[0], -pair[1]))
@@ -335,7 +425,7 @@
                 device_id_type=MESH,
             ).start()
 
-    counts = {"side": (n_side, (1, 2)), "rims": (n_rims, (1, 2, 3, 4, 6)), "wide": (n_wide, (1, 2, 3, 5, 7, 8, 9, 11, 14))}
+    counts = {"side": (n_side, (1, 2)), "rows": (near_y, (1, 2)), "edge": (near_x * near_y, (1, 2, 4)), "rims": (n_rims, (1, 2, 3, 4, 6)), "wide": (n_wide, (1, 2, 3, 5, 7, 8, 9, 11, 14)), "reach": (n_reach, (7, 9, 11, 13, 14, 17, 20))}
 
     def settle(kind, landing, group, sent):
         count, options = counts[kind]
@@ -400,15 +490,40 @@
     w = in_order(coef) * table
     weighted[...] = w
     loads[1].wait()
-    pair = halves(w)
-    diagonal = rows_of(dot(early_part("square_xy"), stacked(pair)))
-    field[1] = fold(diagonal + times_right(pair, early_part("square_z")))
     loads[2].wait()
     field[0] = fold(in_order(rhs))
+    w4 = w.reshape(4, 8, 8, 128)
+    planes = [w4[:, a].reshape(32, 128) for a in range(8)]
+    for side in range(2):
+        one, two = face_moments(7 * side)
+        rows = [weighted[pl.ds(192 * side + b, 8, stride=8), :] for b in range(8)]
+        fside[side, 0:32] = sum(float(one[a]) * planes[a] for a in range(8))
+        fside[side, 32:64] = sum(float(two[a]) * planes[a] for a in range(8))
+        fside[side, 64:96] = planes[7 * side]
+        frow[side, 0] = sum(float(one[b]) * rows[b] for b in range(8))
+        frow[side, 1] = sum(float(two[b]) * rows[b] for b in range(8))
+        frow[side, 2] = rows[7 * side]
+    fedge[...] = jnp.zeros_like(fedge)
+    for at, (dx, dy) in enumerate(EDGE):
+        x_side, y_side = (dx + 1) // 2, (dy + 1) // 2
+        spot, line = 31 * y_side, 7 * x_side
+        fedge[at, 0:1] = 2.0 * (fside[x_side, spot : spot + 1] + frow[y_side, 0, line : line + 1])
+        fedge[at, 1:2] = 2.0 * fside[x_side, 32 + spot : 33 + spot]
+        fedge[at, 2:3] = 2.0 * frow[y_side, 1, line : line + 1]
+        fedge[at, 3:4] = 4.0 * frow[y_side, 2, line : line + 1]
+    pair = halves(w)
+    diagonal = rows_of(dot(early_part("square_xy")[:, 0:192], stacked(pair)))
+    field[1] = fold(diagonal + times_right(pair, early_part("square_z")))
     pack(field, 2, xs1, vs1)
 
-    pl.semaphore_wait(barrier, n_wide)
+    pl.semaphore_wait(barrier, n_reach)
     exchange(xs1, vs1, xr1, vr1, 0)
+    for at, pair in enumerate(SIDE):
+        send(SIDE, pair, fside.at[at], fx, 2)
+    for at, pair in enumerate(ROWS):
+        send(ROWS, pair, frow.at[at], fy, 3)
+    for at, pair in enumerate(EDGE):
+        send(EDGE, pair, fedge.at[at], fe, 4)
 
     loads[3].wait()
     w4 = weighted[...].reshape(4, 8, 8, 128)
@@ -428,20 +543,20 @@
         pmine[at] = one
         mine.append(one.reshape(3, 8, 128))
     dtile[...] = jnp.where(lane8 < 32, mine[0][1], pltpu.roll(mine[2][1], 32, 1))
-    for tile, vertex, first in ((0, 0, 1), (1, 4, 0)):
+    for side, vertex, first in ((0, 0, 1), (1, 4, 0)):
         total = jnp.zeros((8, 128), F32)
         for c in range(3):
             for d in range(2):
                 goal = 2 * c + d
                 moved = pltpu.roll(mine[c][first + d], (goal - vertex) % 8, 0)
                 total = jnp.where(sub8 == goal, moved, total)
-        ptile[tile] = total
-    send(SIDE, (-1, 0), pmine.at[pl.ds(0, 2)], px, 2)
-    send(SIDE, (1, 0), pmine.at[pl.ds(1, 2)], px, 2)
+        ptile[side] = total
+    send(SIDE, (-1, 0), pmine.at[pl.ds(0, 2)], px, 5)
+    send(SIDE, (1, 0), pmine.at[pl.ds(1, 2)], px, 5)
     for pair in RIMS:
-        send(RIMS, pair, ptile.at[0 if pair[1] < 0 else 1], pt, 3)
+        send(RIMS, pair, ptile.at[(pair[1] + 1) // 2], pt, 6)
     for pair in WIDE:
-        send(WIDE, pair, dtile, dr, 4)
+        send(WIDE, pair, dtile, dr, 7)
     loads[4].wait()
 
     settle("side", xr1, 0, False)
@@ -461,12 +576,59 @@
     step[...] = step_one
     held[0] = fold(local_operator(step_one))
     pack(held, 1, xs2, vs2)
-    exchange(xs2, vs2, xr2, vr2, 5)
-
-    settle("side", px, 2, False)
-    settle("rims", pt, 3, False)
-    settle("wide", dr, 4, False)
-
+    exchange(xs2, vs2, xr2, vr2, 8)
+
+    factor = 2.0 * rho1 / delta
+    g = factor * inverse[...] * held[0]
+    gfield[...] = g
+    start = (1.0 + rho1 * rho0) * step_one + factor * inv * residual
+    step[...] = start
+    settle("side", fx, 2, False)
+    settle("rows", fy, 3, False)
+    settle("edge", fe, 4, False)
+    faces = []
+    for first in (0, 56):
+        for j in range(4):
+            faces.append(g[64 * j + first : 64 * j + first + 8])
+    rims = [gfield[pl.ds(0, 8, stride=8), :], gfield[pl.ds(199, 8, stride=8), :]]
+    corner = jnp.zeros((8, 128), F32)
+    lines = [jnp.zeros((8, 128), F32) for _ in range(4)]
+    for at, (dx, dy) in enumerate(EDGE):
+        line = 0 if dx < 0 else 7
+        moved = pltpu.roll(rims[(dy + 1) // 2], (at - line) % 8, 0)
+        corner = jnp.where(sub8 == at, moved, corner)
+        given = fe[at]
+        for k in range(4):
+            lines[k] = jnp.where(sub8 == at, pltpu.roll(given, (at - k) % 8, 0), lines[k])
+    none40 = jnp.zeros((40, 128), F32)
+    faces = jnp.concatenate(faces + rims + [corner, none40], axis=0)
+    two = [2.0 * fx[0, 64:96], 2.0 * fx[1, 64:96], 2.0 * fy[0, 2], 2.0 * fy[1, 2]]
+    w_rows = jnp.concatenate(two + [jnp.zeros((48, 128), F32)], axis=0)
+    w_z = jnp.concatenate(two + [lines[3], none40], axis=0)
+    image, face_image = with_faces(start - g, faces, w_rows, w_z)
+    defect = residual - fmult[...] * image
+    near_w = [fx[0, 0:32], fx[1, 0:32], fy[0, 0], fy[1, 0], lines[0]]
+    far_w = [fx[0, 32:64], fx[1, 32:64], fy[0, 1], fy[1, 1]]
+    near = jnp.concatenate(near_w, axis=0) * faces[0:88] + face_image[0:88]
+    far = jnp.concatenate(far_w, axis=0) * faces[0:80]
+    parts = [
+        near[0:64], far[0:64], near[64:80], far[64:80], near[80:88],
+        lines[1] * corner, lines[2] * corner, jnp.zeros((72, 128), F32),
+    ]
+    twice_z = jnp.where(((lane8 & 7) == 0) | ((lane8 & 7) == 7), 2.0, 1.0)
+    parts = jnp.concatenate(parts, axis=0).reshape(32, 8, 128) * twice_z[None]
+    part = dot(late_part("rest_xy"), jnp.concatenate(halves(defect), axis=1))
+    part = part + dot(late_part("spill"), jnp.concatenate(halves(parts.reshape(256, 128)), axis=1))
+    part = part[0:32, :128] + part[0:32, 128:] + part[32:64, :128]
+    coarse = times_right(halves(part), late_part("rest_z"))
+    tile = jnp.where(lane8 < 64, jnp.where(lane8 < 32, coarse[0:8], coarse[8:16]), jnp.where(lane8 < 96, coarse[16:24], coarse[24:32]))
+    ctile[...] = tile
+    for pair in sorted(REACH, key=lambda p: -abs(p[0]) - abs(p[1])):
+        send(REACH, pair, ctile, cr, 10)
+
+    settle("side", px, 5, False)
+    settle("rims", pt, 6, False)
+    settle("wide", dr, 7, False)
     row_low = sub8 < 2
     row_mid = sub8 == 2
 
@@ -521,33 +683,35 @@
     for v in range(4):
         stencil[18 + v] = scales[v]
 
-    settle("side", xr2, 5, False)
-    settle("rims", vr2, 6, False)
+    settle("side", xr2, 8, False)
+    settle("rims", vr2, 9, False)
     unpack(held, 1, xr2, vr2)
-    residual = field[0]
-    step_one = step[...]
-    res_one = residual - fmask[...] * held[0]
-    second = (1.0 + rho1 * rho0) * step_one + (2.0 * rho1 / delta) * inverse[...] * res_one
-    step[...] = second
-
-    defect = residual - fmult[...] * local_operator(second)
-    part = dot(late_part("rest_xy"), jnp.concatenate(halves(defect), axis=1))
-    part = part[0:16, :128] + part[0:16, 128:] + part[16:32, :128]
-    coarse = times_right(halves(part), late_part("rest_z"))
-    ctile[...] = jnp.where(lane8 < 32, coarse[0:8], coarse[8:16])
-    for pair in sorted(WIDE, key=lambda p: -abs(p[0]) - abs(p[1])):
-        send(WIDE, pair, ctile, cr, 7)
+    step[...] = step[...] - factor * inverse[...] * held[0]
 
     settle("side", xr1, 0, True)
     settle("rims", vr1, 1, True)
-    settle("side", px, 2, True)
-    settle("rims", pt, 3, True)
-    settle("wide", dr, 4, True)
-    settle("side", xr2, 5, True)
-    settle("rims", vr2, 6, True)
-    settle("wide", cr, 7, False)
-
-    ext_rhs = extend(ctile[...], cr)
+    settle("side", fx, 2, True)
+    settle("rows", fy, 3, True)
+    settle("edge", fe, 4, True)
+    settle("side", px, 5, True)
+    settle("rims", pt, 6, True)
+    settle("wide", dr, 7, True)
+    settle("side", xr2, 8, True)
+    settle("rims", vr2, 9, True)
+    settle("reach", cr, 10, False)
+
+    moved = {}
+    mid_rows = (sub8 > 3) & (sub8 < 7)
+    for dx in range(-3, 4):
+        mid = ctile[...] if dx == 0 else cr[REACH.index((dx, 0))]
+        below = cr[REACH.index((dx, -1))]
+        above = cr[REACH.index((dx, 1))]
+        rim = jnp.where(sub8 < 3, above, jnp.where(mid_rows, below, 0.0))
+        moved[dx] = mid + pltpu.roll(rim, 4, 0)
+    whole = moved[0] + pltpu.roll(jnp.where(lane8 < 96, moved[1], moved[-3]), 32, 1)
+    whole = whole + pltpu.roll(jnp.where(lane8 < 64, moved[2], moved[-2]), 64, 1)
+    whole = whole + pltpu.roll(jnp.where(lane8 >= 32, moved[-1], moved[3]), 96, 1)
+    ext_rhs = [whole] + [pltpu.roll(whole, 128 - 32 * v, 1) for v in (1, 2, 3)]
     scales = [stencil[18 + v] for v in range(4)]
     ones = [scales[v] * ext_rhs[v] for v in range(4)]
     packed = [c + pltpu.roll(c, 31, 1) + pltpu.roll(c, 65, 1) for c in ones]
@@ -565,17 +729,17 @@
         results.append(one + scale * (right - image))
     pair = halves(jnp.concatenate(results, axis=0))
     nodes = halves(times_right(pair, late_part("prol_z")))
-    nodes = jnp.concatenate([nodes[0], nodes[0], nodes[1], nodes[1]], axis=0)
-    fine = step[...] + fmask[...] * dot(late_part("prol_xy")[:, 0:64], nodes)
+    nodes = jnp.concatenate([nodes[0], nodes[0], nodes[1]], axis=0)
+    fine = step[...] + fmask[...] * dot(late_part("prol_xy")[:, 0:48], nodes)
     fine = fine.reshape(4, 8, 8, 128)
     for j in range(4):
         out_ref[:, 8 * j : 8 * j + 8, :] = fine[j]
     copies = halves(dot(jnp.concatenate(pair, axis=1), late_part("copy_z")[:, 0:128]))
-    copies = jnp.concatenate([copies[0], copies[0], copies[1], copies[1]], axis=0)
-    copies = dot(late_part("copy_y")[:, 0:64], copies)
+    copies = jnp.concatenate([copies[0], copies[0], copies[1]], axis=0)
+    copies = dot(late_part("copy_y")[:, 0:48], copies)
     coarse_ref[...] = copies.reshape(2, 8, 128)[:, :, 0:32]
 
-    settle("wide", cr, 7, True)
+    settle("reach", cr, 10, True)
 
 
 def finish(fine, coarse, fine_out, coarse_out, sem):
@@ -631,6 +795,10 @@
                 space(8, 128),
                 space(8, 128),
                 space(22, 8, 128),
+                space(256, 128),
+                space(2, 96, 128),
+                space(2, 3, 8, 128),
+                space(4, 8, 128),
                 space(2, 2, 32, 128),
                 space(6, 2, 8, 128),
                 space(2, 1, 32, 128),
@@ -642,10 +810,13 @@
                 space(2, 2, 24, 128),
                 space(6, 8, 128),
                 space(14, 8, 128),
-                space(14, 8, 128),
+                space(20, 8, 128),
+                space(2, 96, 128),
+                space(2, 3, 8, 128),
+                space(4, 8, 128),
                 dma((5,)),
-                dma((8,)),
-                dma((8,)),
+                dma((11,)),
+                dma((11,)),
             ],
             compiler_params=pltpu.CompilerParams(
                 collective_id=0, has_side_effects=True, vmem_limit_bytes=8 * 2**20

time: 28.1 us -> 26.1 us (0.929)
  Pallas kernels: 27.3 us -> 25.3 us
    pallas_call x1, Pallas kernels: 26.6 us -> 24.6 us  [shards(): pl.pallas_call(functools.partial(kernel, (early_at, late_at, flat_at), n_...]
where the time goes in v3:
time: 26.1 us; the launch traced here: 25.9 us
  Pallas kernels  25.3 us (97%)
  between operations  0.64 us (2%)
    pallas_call x1, Pallas kernels, shards(): pl.pallas_call(functools.partial(kernel, (early_at, late_at, flat_at), n_...  24.6 us
    pallas_call x1, Pallas kernels, shards(): pl.pallas_call(finish, out_shape=outs, in_specs=[vmem, vmem], out_specs=(...  0.68 us

profile of v3, /device:TPU:1, one launch (start us, length us, event | category | flops | bytes accessed | tf_op | source)
XLA Modules:
  0.0 25.9 jit_solution(113082253635136535)
XLA Ops:
  0.6 24.6 %shard_map.320 = (f32[8,32,128]{2,1,0:T(8,128)S(1)}, f32[2,8,32]{2,1,0:T(8,128)S(1)}) custom-call(f32[8,32,128]{2,1,0:T(8,128)} %coef_hbm.1, f32[8,32,128]{2,1,0:T(8,128)} %rhs_hbm.1, bf16[320,256]{1,0:T(8,128)(2,1)} %constant.94.early_hbm, bf16[1872,256]{1,0:T(8,128)(2,1)} %constant.160.late_hbm, f32[304,128]{1,0:T(8,128)} %constant.161.flat_hbm), custom_call_target="tpu_custom_call" | custom-call | tf_op jit(solution)/shard_map/pallas_call | solution.py:775
  25.3 0.7 %shard_map.321 = (f32[8,32,128]{2,1,0:T(8,128)}, f32[2,8,32]{2,1,0:T(8,128)}) custom-call(f32[8,32,128]{2,1,0:T(8,128)S(1)} %get-tuple-element.4.fine, f32[2,8,32]{2,1,0:T(8,128)S(1)} %get-tuple-element.5.coarse), custom_call_target="tpu_custom_call" | custom-call | tf_op jit(solution)/shard_map/pallas_call | solution.py:825

commit v4 on v3

--- a/solution.py
+++ b/solution.py
@@ -253,7 +253,7 @@
     pmine, ptile, dtile, ctile, stencil, gfield, fside, frow, fedge,
     xs1, vs1, xs2, vs2,
     xr1, vr1, xr2, vr2, px, pt, dr, cr, fx, fy, fe,
-    load_sem, s_sem, r_sem,
+    load_sem, s_sem, r_sem, ready,
 ):
     early_at, late_at, flat_at = tables_at
     dom = lax.axis_index("dom")
@@ -287,7 +287,7 @@
         buffer[...] = jnp.zeros_like(buffer)
 
     barrier = pltpu.get_barrier_semaphore()
-    for pair in sorted(REACH, key=lambda p: abs(p[0]) + abs(p[1])):
+    for pair in NEAR:
 
         @pl.when(present(pair))
         def _(pair=pair):
@@ -516,8 +516,19 @@
     field[1] = fold(diagonal + times_right(pair, early_part("square_z")))
     pack(field, 2, xs1, vs1)
 
-    pl.semaphore_wait(barrier, n_reach)
+    pl.semaphore_wait(barrier, (1 + near_x) * (1 + near_y) - 1)
     exchange(xs1, vs1, xr1, vr1, 0)
+
+    def announce(stage):
+        for pair in SIDE:
+
+            @pl.when(present(pair))
+            def _(pair=pair):
+                pl.semaphore_signal(
+                    ready.at[stage], inc=1, device_id=target(pair), device_id_type=MESH
+                )
+
+    announce(0)
     for at, pair in enumerate(SIDE):
         send(SIDE, pair, fside.at[at], fx, 2)
     for at, pair in enumerate(ROWS):
@@ -555,6 +566,8 @@
     send(SIDE, (1, 0), pmine.at[pl.ds(1, 2)], px, 5)
     for pair in RIMS:
         send(RIMS, pair, ptile.at[(pair[1] + 1) // 2], pt, 6)
+    pl.semaphore_wait(ready.at[0], near_x)
+    announce(1)
     for pair in WIDE:
         send(WIDE, pair, dtile, dr, 7)
     loads[4].wait()
@@ -623,6 +636,7 @@
     coarse = times_right(halves(part), late_part("rest_z"))
     tile = jnp.where(lane8 < 64, jnp.where(lane8 < 32, coarse[0:8], coarse[8:16]), jnp.where(lane8 < 96, coarse[16:24], coarse[24:32]))
     ctile[...] = tile
+    pl.semaphore_wait(ready.at[1], near_x)
     for pair in sorted(REACH, key=lambda p: -abs(p[0]) - abs(p[1])):
         send(REACH, pair, ctile, cr, 10)
 
@@ -817,6 +831,7 @@
                 dma((5,)),
                 dma((11,)),
                 dma((11,)),
+                pltpu.SemaphoreType.REGULAR((2,)),
             ],
             compiler_params=pltpu.CompilerParams(
                 collective_id=0, has_side_effects=True, vmem_limit_bytes=8 * 2**20

time: 26.1 us -> 24.8 us (0.950)
  Pallas kernels: 25.3 us -> 24 us
    pallas_call x1, Pallas kernels: 24.6 us -> 23.4 us  [shards(): pl.pallas_call(functools.partial(kernel, (early_at, late_at, flat_at), n_...]
where the time goes in v4:
time: 24.8 us; the launch traced here: 24.7 us
  Pallas kernels  24 us (97%)
  between operations  0.64 us (3%)
    pallas_call x1, Pallas kernels, shards(): pl.pallas_call(functools.partial(kernel, (early_at, late_at, flat_at), n_...  23.4 us
    pallas_call x1, Pallas kernels, shards(): pl.pallas_call(finish, out_shape=outs, in_specs=[vmem, vmem], out_specs=(...  0.68 us

profile of v4, /device:TPU:1, one launch (start us, length us, event | category | flops | bytes accessed | tf_op | source)
XLA Modules:
  0.0 24.7 jit_solution(7454247534350588395)
XLA Ops:
  0.6 23.4 %shard_map.320 = (f32[8,32,128]{2,1,0:T(8,128)S(1)}, f32[2,8,32]{2,1,0:T(8,128)S(1)}) custom-call(f32[8,32,128]{2,1,0:T(8,128)} %coef_hbm.1, f32[8,32,128]{2,1,0:T(8,128)} %rhs_hbm.1, bf16[320,256]{1,0:T(8,128)(2,1)} %constant.94.early_hbm, bf16[1872,256]{1,0:T(8,128)(2,1)} %constant.160.late_hbm, f32[304,128]{1,0:T(8,128)} %constant.161.flat_hbm), custom_call_target="tpu_custom_call" | custom-call | tf_op jit(solution)/shard_map/pallas_call | solution.py:789
  24.0 0.7 %shard_map.321 = (f32[8,32,128]{2,1,0:T(8,128)}, f32[2,8,32]{2,1,0:T(8,128)}) custom-call(f32[8,32,128]{2,1,0:T(8,128)S(1)} %get-tuple-element.4.fine, f32[2,8,32]{2,1,0:T(8,128)S(1)} %get-tuple-element.5.coarse), custom_call_target="tpu_custom_call" | custom-call | tf_op jit(solution)/shard_map/pallas_call | solution.py:840

commit v5 on v4

--- a/solution.py
+++ b/solution.py
@@ -364,8 +364,13 @@
         return flat[start : start + count, :]
 
     def times_right(pair, matrix):
-        both = dot(jnp.concatenate(pair, axis=1), matrix)
-        return both[:, :128] + both[:, 128:]
+        left = jnp.concatenate(pair, axis=1)
+        half = left.shape[0] // 2 if left.shape[0] > 32 else left.shape[0]
+        sums = []
+        for at in range(0, left.shape[0], half):
+            both = dot(left[at : at + half], matrix)
+            sums.append(both[:, :128] + both[:, 128:])
+        return jnp.concatenate(sums, axis=0)
 
     def stacked(pair):
         high, low = [
@@ -389,12 +394,16 @@
             planes[7 - a] = q - p
         return jnp.stack(planes, axis=1).reshape(256, 128)
 
-    def with_faces(u, faces, w_rows, w_z):
+    def with_faces(u, faces, face_weights):
         w = weighted[...]
         pair = halves(jnp.concatenate([u, faces], axis=0))
         both = dot(late_part("grad_xy")[:, 0:192], stacked(pair))
         all_z = times_right(pair, late_part("grad_z"))
         all_y = rows_of(both[64:128])
+        settle("side", fx, 2, False)
+        settle("rows", fy, 3, False)
+        settle("edge", fe, 4, False)
+        w_rows, w_z = face_weights()
         flux_z = halves(jnp.concatenate([w * all_z[0:256], w_z * all_z[256:384]], axis=0))
         flux_y = halves(jnp.concatenate([w * all_y[0:256], w_rows * all_y[256:384]], axis=0))
         back = rows_of(dot(late_part("back_y")[:, 0:192], stacked(flux_y)))
@@ -596,29 +605,31 @@
     gfield[...] = g
     start = (1.0 + rho1 * rho0) * step_one + factor * inv * residual
     step[...] = start
-    settle("side", fx, 2, False)
-    settle("rows", fy, 3, False)
-    settle("edge", fe, 4, False)
     faces = []
     for first in (0, 56):
         for j in range(4):
             faces.append(g[64 * j + first : 64 * j + first + 8])
     rims = [gfield[pl.ds(0, 8, stride=8), :], gfield[pl.ds(199, 8, stride=8), :]]
     corner = jnp.zeros((8, 128), F32)
-    lines = [jnp.zeros((8, 128), F32) for _ in range(4)]
     for at, (dx, dy) in enumerate(EDGE):
         line = 0 if dx < 0 else 7
         moved = pltpu.roll(rims[(dy + 1) // 2], (at - line) % 8, 0)
         corner = jnp.where(sub8 == at, moved, corner)
-        given = fe[at]
-        for k in range(4):
-            lines[k] = jnp.where(sub8 == at, pltpu.roll(given, (at - k) % 8, 0), lines[k])
     none40 = jnp.zeros((40, 128), F32)
     faces = jnp.concatenate(faces + rims + [corner, none40], axis=0)
-    two = [2.0 * fx[0, 64:96], 2.0 * fx[1, 64:96], 2.0 * fy[0, 2], 2.0 * fy[1, 2]]
-    w_rows = jnp.concatenate(two + [jnp.zeros((48, 128), F32)], axis=0)
-    w_z = jnp.concatenate(two + [lines[3], none40], axis=0)
-    image, face_image = with_faces(start - g, faces, w_rows, w_z)
+    lines = []
+
+    def face_weights():
+        for k in range(4):
+            one = jnp.zeros((8, 128), F32)
+            for at in range(4):
+                one = jnp.where(sub8 == at, pltpu.roll(fe[at], (at - k) % 8, 0), one)
+            lines.append(one)
+        two = [2.0 * fx[0, 64:96], 2.0 * fx[1, 64:96], 2.0 * fy[0, 2], 2.0 * fy[1, 2]]
+        w_rows = jnp.concatenate(two + [jnp.zeros((48, 128), F32)], axis=0)
+        return w_rows, jnp.concatenate(two + [lines[3], none40], axis=0)
+
+    image, face_image = with_faces(start - g, faces, face_weights)
     defect = residual - fmult[...] * image
     near_w = [fx[0, 0:32], fx[1, 0:32], fy[0, 0], fy[1, 0], lines[0]]
     far_w = [fx[0, 32:64], fx[1, 32:64], fy[0, 1], fy[1, 1]]

time: 24.8 us -> 24.9 us (level)
  no operation moved by 1% of the time
where the time goes in v5:
time: 24.9 us; the launch traced here: 24.8 us
  Pallas kernels  24.1 us (97%)
  between operations  0.64 us (3%)
    pallas_call x1, Pallas kernels, shards(): pl.pallas_call(functools.partial(kernel, (early_at, late_at, flat_at), n_...  23.4 us
    pallas_call x1, Pallas kernels, shards(): pl.pallas_call(finish, out_shape=outs, in_specs=[vmem, vmem], out_specs=(...  0.68 us

profile of v5, /device:TPU:1, one launch (start us, length us, event | category | flops | bytes accessed | tf_op | source)
XLA Modules:
  0.0 24.8 jit_solution(34498071678807000)
XLA Ops:
  0.6 23.4 %shard_map.320 = (f32[8,32,128]{2,1,0:T(8,128)S(1)}, f32[2,8,32]{2,1,0:T(8,128)S(1)}) custom-call(f32[8,32,128]{2,1,0:T(8,128)} %coef_hbm.1, f32[8,32,128]{2,1,0:T(8,128)} %rhs_hbm.1, bf16[320,256]{1,0:T(8,128)(2,1)} %constant.94.early_hbm, bf16[1872,256]{1,0:T(8,128)(2,1)} %constant.160.late_hbm, f32[304,128]{1,0:T(8,128)} %constant.161.flat_hbm), custom_call_target="tpu_custom_call" | custom-call | tf_op jit(solution)/shard_map/pallas_call | solution.py:800
  24.1 0.7 %shard_map.321 = (f32[8,32,128]{2,1,0:T(8,128)}, f32[2,8,32]{2,1,0:T(8,128)}) custom-call(f32[8,32,128]{2,1,0:T(8,128)S(1)} %get-tuple-element.4.fine, f32[2,8,32]{2,1,0:T(8,128)S(1)} %get-tuple-element.5.coarse), custom_call_target="tpu_custom_call" | custom-call | tf_op jit(solution)/shard_map/pallas_call | solution.py:851

commit v6 on v4

--- a/solution.py
+++ b/solution.py
@@ -251,8 +251,8 @@
     out_ref, coarse_ref,
     coef, rhs, early, late, flat, weighted, field, held, fmask, fmult, inverse, step,
     pmine, ptile, dtile, ctile, stencil, gfield, fside, frow, fedge,
-    xs1, vs1, xs2, vs2,
-    xr1, vr1, xr2, vr2, px, pt, dr, cr, fx, fy, fe,
+    xs1, vs1, es1, xs2, vs2, es2,
+    xr1, vr1, er1, xr2, vr2, er2, px, pt, dr, cr, fx, fy, fe,
     load_sem, s_sem, r_sem, ready,
 ):
     early_at, late_at, flat_at = tables_at
@@ -283,7 +283,7 @@
     def target(pair):
         return (dom + pair[0], sub + pair[1])
 
-    for buffer in (xr1, vr1, xr2, vr2, px, pt, dr, cr, fx, fy, fe):
+    for buffer in (xr1, vr1, er1, xr2, vr2, er2, px, pt, dr, cr, fx, fy, fe):
         buffer[...] = jnp.zeros_like(buffer)
 
     barrier = pltpu.get_barrier_semaphore()
@@ -446,40 +446,39 @@
                 else:
                     copy.wait_recv()
 
-    def pack(refs, fields, xs, vs):
+    def pack(refs, fields, xs, vs, es):
         for f in range(fields):
             ref = refs.at[f]
             faces = {-1: ref[pl.ds(0, 8, stride=8), :], 1: ref[pl.ds(199, 8, stride=8), :]}
             for j in range(4):
                 xs[0, f, 8 * j : 8 * j + 8] = ref[64 * j : 64 * j + 8, :]
                 xs[1, f, 8 * j : 8 * j + 8] = ref[64 * j + 56 : 64 * j + 64, :]
-            for at, (dx, dy) in enumerate(RIMS):
-                face = faces[dy]
-                if dx < 0:
-                    face = jnp.where(sub8 == 7, pltpu.roll(face, 7, 0), 0.0)
-                if dx > 0:
-                    face = jnp.where(sub8 == 0, pltpu.roll(face, 1, 0), 0.0)
-                vs[at, f] = face
-
-    def exchange(xs, vs, xr, vr, group):
-        for pair in RIMS:
-            if pair[0] != 0:
-                send(RIMS, pair, vs.at[RIMS.index(pair)], vr, group + 1)
+            for at, (_, dy) in enumerate(ROWS):
+                vs[at, f] = faces[dy]
+            for at, (dx, dy) in enumerate(EDGE):
+                line = 0 if dx < 0 else 7
+                es[at, f] = faces[dy][line : line + 1]
+
+    def exchange(xs, vs, es, xr, vr, er, group, edge_group):
+        for pair in EDGE:
+            send(EDGE, pair, es.at[EDGE.index(pair)], er, edge_group)
         for pair in SIDE:
             send(SIDE, pair, xs.at[SIDE.index(pair)], xr, group)
-        for pair in RIMS:
-            if pair[0] == 0:
-                send(RIMS, pair, vs.at[RIMS.index(pair)], vr, group + 1)
-
-    def unpack(refs, fields, xr, vr):
+        for pair in ROWS:
+            send(ROWS, pair, vs.at[ROWS.index(pair)], vr, group + 1)
+
+    def unpack(refs, fields, xr, vr, er):
         for f in range(fields):
             ref = refs.at[f]
             for j in range(4):
                 ref[64 * j : 64 * j + 8, :] += xr[0, f, 8 * j : 8 * j + 8]
                 ref[64 * j + 56 : 64 * j + 64, :] += xr[1, f, 8 * j : 8 * j + 8]
             for dy, start in ((-1, 0), (1, 199)):
-                a, b, c = [vr[RIMS.index((dx, dy)), f] for dx in (-1, 0, 1)]
-                ref[pl.ds(start, 8, stride=8), :] += a + b + c
+                extra = vr[ROWS.index((0, dy)), f]
+                low = er[EDGE.index((-1, dy)), f]
+                high = er[EDGE.index((1, dy)), f]
+                extra = extra + jnp.where(sub8 == 0, low, jnp.where(sub8 == 7, high, 0.0))
+                ref[pl.ds(start, 8, stride=8), :] += extra
 
     def in_order(ref):
         v = ref[...].reshape(8, 4, 8, 128)
@@ -514,10 +513,10 @@
     pair = halves(w)
     diagonal = rows_of(dot(early_part("square_xy")[:, 0:192], stacked(pair)))
     field[1] = fold(diagonal + times_right(pair, early_part("square_z")))
-    pack(field, 2, xs1, vs1)
+    pack(field, 2, xs1, vs1, es1)
 
     pl.semaphore_wait(barrier, (1 + near_x) * (1 + near_y) - 1)
-    exchange(xs1, vs1, xr1, vr1, 0)
+    exchange(xs1, vs1, es1, xr1, vr1, er1, 0, 11)
 
     def announce(stage):
         for pair in SIDE:
@@ -573,8 +572,9 @@
     loads[4].wait()
 
     settle("side", xr1, 0, False)
-    settle("rims", vr1, 1, False)
-    unpack(field, 2, xr1, vr1)
+    settle("rows", vr1, 1, False)
+    settle("edge", er1, 11, False)
+    unpack(field, 2, xr1, vr1, er1)
 
     residual = fmask[...] * field[0]
     inv = fmask[...] / field[1]
@@ -588,8 +588,8 @@
     step_one = inv * residual / theta
     step[...] = step_one
     held[0] = fold(local_operator(step_one))
-    pack(held, 1, xs2, vs2)
-    exchange(xs2, vs2, xr2, vr2, 8)
+    pack(held, 1, xs2, vs2, es2)
+    exchange(xs2, vs2, es2, xr2, vr2, er2, 8, 12)
 
     factor = 2.0 * rho1 / delta
     g = factor * inverse[...] * held[0]
@@ -698,12 +698,14 @@
         stencil[18 + v] = scales[v]
 
     settle("side", xr2, 8, False)
-    settle("rims", vr2, 9, False)
-    unpack(held, 1, xr2, vr2)
+    settle("rows", vr2, 9, False)
+    settle("edge", er2, 12, False)
+    unpack(held, 1, xr2, vr2, er2)
     step[...] = step[...] - factor * inverse[...] * held[0]
 
     settle("side", xr1, 0, True)
-    settle("rims", vr1, 1, True)
+    settle("rows", vr1, 1, True)
+    settle("edge", er1, 11, True)
     settle("side", fx, 2, True)
     settle("rows", fy, 3, True)
     settle("edge", fe, 4, True)
@@ -711,7 +713,8 @@
     settle("rims", pt, 6, True)
     settle("wide", dr, 7, True)
     settle("side", xr2, 8, True)
-    settle("rims", vr2, 9, True)
+    settle("rows", vr2, 9, True)
+    settle("edge", er2, 12, True)
     settle("reach", cr, 10, False)
 
     moved = {}
@@ -814,13 +817,17 @@
                 space(2, 3, 8, 128),
                 space(4, 8, 128),
                 space(2, 2, 32, 128),
-                space(6, 2, 8, 128),
+                space(2, 2, 8, 128),
+                space(4, 2, 1, 128),
                 space(2, 1, 32, 128),
-                space(6, 1, 8, 128),
+                space(2, 1, 8, 128),
+                space(4, 1, 1, 128),
                 space(2, 2, 32, 128),
-                space(6, 2, 8, 128),
+                space(2, 2, 8, 128),
+                space(4, 2, 1, 128),
                 space(2, 1, 32, 128),
-                space(6, 1, 8, 128),
+                space(2, 1, 8, 128),
+                space(4, 1, 1, 128),
                 space(2, 2, 24, 128),
                 space(6, 8, 128),
                 space(14, 8, 128),
@@ -829,8 +836,8 @@
                 space(2, 3, 8, 128),
                 space(4, 8, 128),
                 dma((5,)),
-                dma((11,)),
-                dma((11,)),
+                dma((13,)),
+                dma((13,)),
                 pltpu.SemaphoreType.REGULAR((2,)),
             ],
             compiler_params=pltpu.CompilerParams(

time: 24.8 us -> 24.7 us (level)
  no operation moved by 1% of the time
where the time goes in v6:
time: 24.7 us; the launch traced here: 24.6 us
  Pallas kernels  23.9 us (97%)
  between operations  0.64 us (3%)
    pallas_call x1, Pallas kernels, shards(): pl.pallas_call(functools.partial(kernel, (early_at, late_at, flat_at), n_...  23.3 us
    pallas_call x1, Pallas kernels, shards(): pl.pallas_call(finish, out_shape=outs, in_specs=[vmem, vmem], out_specs=(...  0.68 us

profile of v6, /device:TPU:1, one launch (start us, length us, event | category | flops | bytes accessed | tf_op | source)
XLA Modules:
  0.0 24.6 jit_solution(12672351989061922211)
XLA Ops:
  0.6 23.3 %shard_map.320 = (f32[8,32,128]{2,1,0:T(8,128)S(1)}, f32[2,8,32]{2,1,0:T(8,128)S(1)}) custom-call(f32[8,32,128]{2,1,0:T(8,128)} %coef_hbm.1, f32[8,32,128]{2,1,0:T(8,128)} %rhs_hbm.1, bf16[320,256]{1,0:T(8,128)(2,1)} %constant.94.early_hbm, bf16[1872,256]{1,0:T(8,128)(2,1)} %constant.160.late_hbm, f32[304,128]{1,0:T(8,128)} %constant.161.flat_hbm), custom_call_target="tpu_custom_call" | custom-call | tf_op jit(solution)/shard_map/pallas_call | solution.py:792
  23.9 0.7 %shard_map.321 = (f32[8,32,128]{2,1,0:T(8,128)}, f32[2,8,32]{2,1,0:T(8,128)}) custom-call(f32[8,32,128]{2,1,0:T(8,128)S(1)} %get-tuple-element.4.fine, f32[2,8,32]{2,1,0:T(8,128)S(1)} %get-tuple-element.5.coarse), custom_call_target="tpu_custom_call" | custom-call | tf_op jit(solution)/shard_map/pallas_call | solution.py:847

commit v7 on v6

--- a/solution.py
+++ b/solution.py
@@ -364,8 +364,13 @@
         return flat[start : start + count, :]
 
     def times_right(pair, matrix):
-        both = dot(jnp.concatenate(pair, axis=1), matrix)
-        return both[:, :128] + both[:, 128:]
+        left = jnp.concatenate(pair, axis=1)
+        half = left.shape[0] // 2 if left.shape[0] > 32 else left.shape[0]
+        sums = []
+        for at in range(0, left.shape[0], half):
+            both = dot(left[at : at + half], matrix)
+            sums.append(both[:, :128] + both[:, 128:])
+        return jnp.concatenate(sums, axis=0)
 
     def stacked(pair):
         high, low = [
@@ -389,12 +394,16 @@
             planes[7 - a] = q - p
         return jnp.stack(planes, axis=1).reshape(256, 128)
 
-    def with_faces(u, faces, w_rows, w_z):
+    def with_faces(u, faces, face_weights):
         w = weighted[...]
         pair = halves(jnp.concatenate([u, faces], axis=0))
         both = dot(late_part("grad_xy")[:, 0:192], stacked(pair))
         all_z = times_right(pair, late_part("grad_z"))
         all_y = rows_of(both[64:128])
+        settle("side", fx, 2, False)
+        settle("rows", fy, 3, False)
+        settle("edge", fe, 4, False)
+        w_rows, w_z = face_weights()
         flux_z = halves(jnp.concatenate([w * all_z[0:256], w_z * all_z[256:384]], axis=0))
         flux_y = halves(jnp.concatenate([w * all_y[0:256], w_rows * all_y[256:384]], axis=0))
         back = rows_of(dot(late_part("back_y")[:, 0:192], stacked(flux_y)))
@@ -596,29 +605,31 @@
     gfield[...] = g
     start = (1.0 + rho1 * rho0) * step_one + factor * inv * residual
     step[...] = start
-    settle("side", fx, 2, False)
-    settle("rows", fy, 3, False)
-    settle("edge", fe, 4, False)
     faces = []
     for first in (0, 56):
         for j in range(4):
             faces.append(g[64 * j + first : 64 * j + first + 8])
     rims = [gfield[pl.ds(0, 8, stride=8), :], gfield[pl.ds(199, 8, stride=8), :]]
     corner = jnp.zeros((8, 128), F32)
-    lines = [jnp.zeros((8, 128), F32) for _ in range(4)]
     for at, (dx, dy) in enumerate(EDGE):
         line = 0 if dx < 0 else 7
         moved = pltpu.roll(rims[(dy + 1) // 2], (at - line) % 8, 0)
         corner = jnp.where(sub8 == at, moved, corner)
-        given = fe[at]
-        for k in range(4):
-            lines[k] = jnp.where(sub8 == at, pltpu.roll(given, (at - k) % 8, 0), lines[k])
     none40 = jnp.zeros((40, 128), F32)
     faces = jnp.concatenate(faces + rims + [corner, none40], axis=0)
-    two = [2.0 * fx[0, 64:96], 2.0 * fx[1, 64:96], 2.0 * fy[0, 2], 2.0 * fy[1, 2]]
-    w_rows = jnp.concatenate(two + [jnp.zeros((48, 128), F32)], axis=0)
-    w_z = jnp.concatenate(two + [lines[3], none40], axis=0)
-    image, face_image = with_faces(start - g, faces, w_rows, w_z)
+    lines = []
+
+    def face_weights():
+        for k in range(4):
+            one = jnp.zeros((8, 128), F32)
+            for at in range(4):
+                one = jnp.where(sub8 == at, pltpu.roll(fe[at], (at - k) % 8, 0), one)
+            lines.append(one)
+        two = [2.0 * fx[0, 64:96], 2.0 * fx[1, 64:96], 2.0 * fy[0, 2], 2.0 * fy[1, 2]]
+        w_rows = jnp.concatenate(two + [jnp.zeros((48, 128), F32)], axis=0)
+        return w_rows, jnp.concatenate(two + [lines[3], none40], axis=0)
+
+    image, face_image = with_faces(start - g, faces, face_weights)
     defect = residual - fmult[...] * image
     near_w = [fx[0, 0:32], fx[1, 0:32], fy[0, 0], fy[1, 0], lines[0]]
     far_w = [fx[0, 32:64], fx[1, 32:64], fy[0, 1], fy[1, 1]]

time: 24.7 us -> 24.8 us (level)
  no operation moved by 1% of the time
where the time goes in v7:
time: 24.8 us; the launch traced here: 24.6 us
  Pallas kernels  24 us (97%)
  between operations  0.64 us (3%)
    pallas_call x1, Pallas kernels, shards(): pl.pallas_call(functools.partial(kernel, (early_at, late_at, flat_at), n_...  23.3 us
    pallas_call x1, Pallas kernels, shards(): pl.pallas_call(finish, out_shape=outs, in_specs=[vmem, vmem], out_specs=(...  0.68 us

profile of v7, /device:TPU:1, one launch (start us, length us, event | category | flops | bytes accessed | tf_op | source)
XLA Modules:
  0.0 24.6 jit_solution(6617152058473598784)
XLA Ops:
  0.6 23.3 %shard_map.320 = (f32[8,32,128]{2,1,0:T(8,128)S(1)}, f32[2,8,32]{2,1,0:T(8,128)S(1)}) custom-call(f32[8,32,128]{2,1,0:T(8,128)} %coef_hbm.1, f32[8,32,128]{2,1,0:T(8,128)} %rhs_hbm.1, bf16[320,256]{1,0:T(8,128)(2,1)} %constant.94.early_hbm, bf16[1872,256]{1,0:T(8,128)(2,1)} %constant.160.late_hbm, f32[304,128]{1,0:T(8,128)} %constant.161.flat_hbm), custom_call_target="tpu_custom_call" | custom-call | tf_op jit(solution)/shard_map/pallas_call | solution.py:803
  24.0 0.7 %shard_map.321 = (f32[8,32,128]{2,1,0:T(8,128)}, f32[2,8,32]{2,1,0:T(8,128)}) custom-call(f32[8,32,128]{2,1,0:T(8,128)S(1)} %get-tuple-element.4.fine, f32[2,8,32]{2,1,0:T(8,128)S(1)} %get-tuple-element.5.coarse), custom_call_target="tpu_custom_call" | custom-call | tf_op jit(solution)/shard_map/pallas_call | solution.py:858

commit v8 on v6

--- a/solution.py
+++ b/solution.py
@@ -287,7 +287,7 @@
         buffer[...] = jnp.zeros_like(buffer)
 
     barrier = pltpu.get_barrier_semaphore()
-    for pair in NEAR:
+    for pair in sorted(NEAR, key=lambda p: -abs(p[0]) - abs(p[1])):
 
         @pl.when(present(pair))
         def _(pair=pair):
@@ -527,13 +527,13 @@
                     ready.at[stage], inc=1, device_id=target(pair), device_id_type=MESH
                 )
 
-    announce(0)
     for at, pair in enumerate(SIDE):
         send(SIDE, pair, fside.at[at], fx, 2)
     for at, pair in enumerate(ROWS):
         send(ROWS, pair, frow.at[at], fy, 3)
     for at, pair in enumerate(EDGE):
         send(EDGE, pair, fedge.at[at], fe, 4)
+    announce(0)
 
     loads[3].wait()
     w4 = weighted[...].reshape(4, 8, 8, 128)

time: 24.7 us -> 24.7 us (level)
  no operation moved by 1% of the time
where the time goes in v8:
time: 24.7 us; the launch traced here: 24.5 us
  Pallas kernels  23.9 us (97%)
  between operations  0.64 us (3%)
    pallas_call x1, Pallas kernels, shards(): pl.pallas_call(functools.partial(kernel, (early_at, late_at, flat_at), n_...  23.2 us
    pallas_call x1, Pallas kernels, shards(): pl.pallas_call(finish, out_shape=outs, in_specs=[vmem, vmem], out_specs=(...  0.68 us

profile of v8, /device:TPU:1, one launch (start us, length us, event | category | flops | bytes accessed | tf_op | source)
XLA Modules:
  0.0 24.5 jit_solution(9299247405604029183)
XLA Ops:
  0.6 23.2 %shard_map.320 = (f32[8,32,128]{2,1,0:T(8,128)S(1)}, f32[2,8,32]{2,1,0:T(8,128)S(1)}) custom-call(f32[8,32,128]{2,1,0:T(8,128)} %coef_hbm.1, f32[8,32,128]{2,1,0:T(8,128)} %rhs_hbm.1, bf16[320,256]{1,0:T(8,128)(2,1)} %constant.94.early_hbm, bf16[1872,256]{1,0:T(8,128)(2,1)} %constant.160.late_hbm, f32[304,128]{1,0:T(8,128)} %constant.161.flat_hbm), custom_call_target="tpu_custom_call" | custom-call | tf_op jit(solution)/shard_map/pallas_call | solution.py:792
  23.9 0.7 %shard_map.321 = (f32[8,32,128]{2,1,0:T(8,128)}, f32[2,8,32]{2,1,0:T(8,128)}) custom-call(f32[8,32,128]{2,1,0:T(8,128)S(1)} %get-tuple-element.4.fine, f32[2,8,32]{2,1,0:T(8,128)S(1)} %get-tuple-element.5.coarse), custom_call_target="tpu_custom_call" | custom-call | tf_op jit(solution)/shard_map/pallas_call | solution.py:847
